TPU v7x, 512 devices: a whole 4x4x16 slice. The times are simulated.
512 devices in a mesh: ctx: 32 (over z_hi, y, core), tp: 16 (over z_lo, x).
Axes of the slice: x: 4, y: 4, z: 16 (z_hi: 4, z_lo: 4; z = z_hi * 4 + z_lo), core: 2. Of those that a mesh axis runs over, the one named last changes fastest.
Arguments:
- lin_q: bfloat16 [64, 8192, 128], P('tp', 'ctx'), may hold values from -6 to 6
- lin_k: bfloat16 [64, 8192, 128], P('tp', 'ctx'), may hold values from -0.5 to 0.5
- lin_v: bfloat16 [64, 8192, 128], P('tp', 'ctx'), may hold values from -6 to 6
- log_decay: float32 [64, 8192], P('tp', 'ctx'), may hold values from -1 to 0
- prior_state: float32 [64, 128, 128], P('tp'), may hold values from -48 to 48
- lin_gain: float32 [64, 128], P('tp'), may hold values from 0.5 to 1.5
- soft_q: bfloat16 [64, 8192, 128], P('tp', 'ctx'), may hold values from -23 to 23
- span_k: bfloat16 [8, 8192, 128], P(None, 'ctx'), may hold values from -4 to 4
- span_v: bfloat16 [8, 8192, 128], P(None, 'ctx'), may hold values from -6 to 6
- cache_k: bfloat16 [8, 4096, 128], P(None, 'ctx'), may hold values from -4 to 4
- cached_value_rows: bfloat16 [8, 4096, 128], P(None, 'ctx'), may hold values from -6 to 6
- cache_len: int32 [32], replicated, may hold values from 2 to 128, as said below
Outputs:
- lightning_normalized_result: bfloat16 [64, 8192, 128], P('tp', 'ctx')
- soft_out: bfloat16 [64, 8192, 128], P('tp', 'ctx')
Inputs may be any that keep to these rules, and one draw needn't show every extreme that they name: Block r holds cache_len[r] live rows from its start; some block is full in every draw.
All inputs are finite; a program needn't handle non-finite values.
Results may differ from a plain program's by a relative error of at most 0.01.
Values may be sent and summed in bfloat16 or wider, within the bound.
No kernel may reach another device: no remote copies, remote signals or barrier semaphores. Data moves between devices by JAX's collectives and lax.ppermute only.
A program may use at most 64 MiB of HBM per device.

v0:
```python
import math

import jax
import jax.numpy as jnp
from jax import lax
from jax.sharding import PartitionSpec as P

HEADS_DEV = 4
GROUP_Q = 8
BLOCK = 256


MASK_FILL = -1e30
HIGHEST_PRECISION = lax.Precision.HIGHEST


def carried_in(shard, axis, join, neutral):
    place = lax.axis_index(axis)
    gathered = jax.tree.map(
        lambda a, kind: lax.all_gather(a.astype(kind), axis), shard, (jnp.bfloat16, jnp.bfloat16)
    )
    state = jax.tree.map(lambda a, e: jnp.zeros_like(a) + jnp.asarray(e, a.dtype), shard, neutral)

    def one(lap, state):
        return join(
            state,
            jax.tree.map(
                lambda a, own: lax.dynamic_index_in_dim(a, lap, 0, False).astype(own.dtype),
                gathered,
                shard,
            ),
        )

    return lax.fori_loop(0, place, one, state)


def split_blocks(array):
    shaped = array.reshape((array.shape[0], array.shape[1] // BLOCK, BLOCK) + array.shape[2:])
    return jnp.moveaxis(shaped, 1, 0)


def join_blocks(array):
    moved = jnp.moveaxis(array, 0, 1)
    return moved.reshape((moved.shape[0], moved.shape[1] * moved.shape[2]) + moved.shape[3:])


def local_blocks(lin_q, lin_k, lin_v, log_decay):
    resident_attention_heads, local_tokens, head_width = lin_q.shape
    offsets = jnp.arange(BLOCK, dtype=jnp.int32)
    causal = (offsets[:, None] >= offsets[None, :])[None]

    def block_step(running, inputs):
        state_now, decay_run = running
        query_part, key_part, value_part, decay_part = inputs
        cumulative = jnp.cumsum(decay_part, axis=1)
        final_sum = cumulative[:, -1:]
        decay_gap = jnp.where(causal, cumulative[:, :, None] - cumulative[:, None, :], 0.0)
        scores = jnp.einsum(
            "hqd,hkd->hqk", query_part, key_part, preferred_element_type=jnp.float32
        )
        weights = jnp.where(causal, scores * jnp.exp(decay_gap), 0.0).astype(jnp.bfloat16)
        intra_part = jnp.einsum(
            "hqk,hkd->hqd", weights, value_part, preferred_element_type=jnp.float32
        )
        query_wide = query_part.astype(jnp.float32)
        inter_part = jnp.exp(cumulative)[:, :, None] * jnp.einsum(
            "hqd,hde->hqe", query_wide, state_now, precision=HIGHEST_PRECISION
        )
        keyed_rows = key_part.astype(jnp.float32) * jnp.exp(final_sum - cumulative)[:, :, None]
        state_next = jnp.exp(final_sum)[:, :, None] * state_now + jnp.einsum(
            "hkd,hke->hde", keyed_rows, value_part.astype(jnp.float32), precision=HIGHEST_PRECISION
        )
        factor = jnp.exp(decay_run[:, None] + cumulative)
        return ((state_next, decay_run + final_sum[:, 0]), (intra_part + inter_part, factor))

    start_state = jnp.zeros((resident_attention_heads, head_width, head_width), jnp.float32)
    start_run = jnp.zeros((resident_attention_heads,), jnp.float32)
    inputs = (
        split_blocks(lin_q),
        split_blocks(lin_k),
        split_blocks(lin_v),
        split_blocks(log_decay),
    )
    (local_state, decay_total), (mixed_blocks, factor_blocks) = lax.scan(
        block_step, (start_state, start_run), inputs
    )
    return (local_state, decay_total, join_blocks(mixed_blocks), join_blocks(factor_blocks))


def per_device(
    lin_q,
    lin_k,
    lin_v,
    log_decay,
    prior_state,
    lin_gain,
    soft_q,
    span_k,
    span_v,
    cache_k,
    cached_value_rows,
    cache_len,
):
    local_state, decay_total, local_mixed, factor = local_blocks(lin_q, lin_k, lin_v, log_decay)

    def combine(earlier, latter):
        return (earlier[0] + latter[0], jnp.exp(latter[0])[:, None, None] * earlier[1] + latter[1])

    identity = (jnp.zeros_like(decay_total), jnp.zeros_like(local_state))
    before, carried = carried_in((decay_total, local_state), "ctx", combine, identity)
    state_in = carried + jnp.exp(before)[:, None, None] * prior_state
    lin_mixed = local_mixed + factor[:, :, None] * jnp.einsum(
        "hqd,hde->hqe", lin_q.astype(jnp.float32), state_in, precision=HIGHEST_PRECISION
    )
    lin_heads, lin_tokens, lin_width = lin_mixed.shape
    square_sums = jnp.sum(lin_mixed * lin_mixed, axis=(0, 2))
    total_squares = lax.psum(square_sums, "tp")
    mean_square = total_squares / (lax.axis_size("tp") * lin_heads * lin_width)
    lightning_normalized_result = (
        lin_mixed * lax.rsqrt(mean_square + 1e-05)[None, :, None] * lin_gain[:, None, :]
    ).astype(jnp.bfloat16)
    resident_attention_heads, local_tokens, head_width = soft_q.shape
    logit_scale = 1.0 / math.sqrt(head_width)
    device_index = lax.axis_index("ctx")
    query_position = device_index * local_tokens + jnp.arange(local_tokens, dtype=jnp.int32)
    last_query = device_index * local_tokens + local_tokens - 1
    kv_head = lax.axis_index("tp") * HEADS_DEV // GROUP_Q
    head_keys = lax.dynamic_index_in_dim(span_k, kv_head, 0, keepdims=False)
    head_values = lax.dynamic_index_in_dim(span_v, kv_head, 0, keepdims=False)
    cache_head_keys = lax.dynamic_index_in_dim(cache_k, kv_head, 0, keepdims=False)
    cache_head_values = lax.dynamic_index_in_dim(cached_value_rows, kv_head, 0, keepdims=False)
    cache_block = cache_k.shape[1]
    block_order = jnp.arange(cache_len.shape[0], dtype=jnp.int32)

    def online_update(running, key_block, value_block, live_mask):
        peak_now, denominator, accumulated = running
        raw_scores = (
            jnp.einsum("hqd,kd->hqk", soft_q, key_block, preferred_element_type=jnp.float32)
            * logit_scale
        )
        scores = jnp.where(live_mask, raw_scores, MASK_FILL)
        upcoming_maximum = jnp.maximum(peak_now, jnp.max(scores, axis=2, keepdims=True))
        probabilities = jnp.where(live_mask, jnp.exp(scores - upcoming_maximum), 0.0)
        rescale = jnp.exp(peak_now - upcoming_maximum)
        denominator = denominator * rescale + jnp.sum(probabilities, axis=2, keepdims=True)
        accumulated = accumulated * rescale + jnp.einsum(
            "hqk,kd->hqd",
            probabilities.astype(jnp.bfloat16),
            value_block,
            preferred_element_type=jnp.float32,
        )
        return (upcoming_maximum, denominator, accumulated)

    def cache_live_rows(cache_rows):
        block_ids = cache_rows // cache_block
        live_lengths = jnp.sum(
            jnp.where(block_ids[:, None] == block_order[None, :], cache_len[None, :], 0), axis=1
        )
        return cache_rows - block_ids * cache_block < live_lengths

    start_carry = (
        jnp.full((resident_attention_heads, local_tokens, 1), MASK_FILL, jnp.float32),
        jnp.zeros((resident_attention_heads, local_tokens, 1), jnp.float32),
        jnp.zeros((resident_attention_heads, local_tokens, head_width), jnp.float32),
    )
    running = start_carry
    key_rows = lax.all_gather(cache_head_keys, "ctx", axis=0, tiled=True)
    value_rows = lax.all_gather(cache_head_values, "ctx", axis=0, tiled=True)
    piece_rows = key_rows.shape[0]
    sub_rows = math.gcd(piece_rows, 512)

    def cache_fold_step(partial_value, step_index):
        first_row = step_index * sub_rows
        key_block = lax.dynamic_slice_in_dim(key_rows, first_row, sub_rows, 0)
        value_block = lax.dynamic_slice_in_dim(value_rows, first_row, sub_rows, 0)
        cache_rows = first_row + jnp.arange(sub_rows, dtype=jnp.int32)
        live_mask = cache_live_rows(cache_rows)[None, None, :]
        return (online_update(partial_value, key_block, value_block, live_mask), None)

    running, _ = lax.scan(
        cache_fold_step, running, jnp.arange(piece_rows // sub_rows, dtype=jnp.int32)
    )
    span_running = running
    span_key_rows = lax.all_gather(head_keys, "ctx", axis=0, tiled=True)
    span_value_rows = lax.all_gather(head_values, "ctx", axis=0, tiled=True)
    piece_rows = span_key_rows.shape[0]
    span_sub_rows = math.gcd(piece_rows, 512)

    def span_fold_step(partial_value, step_index):
        first_row = step_index * span_sub_rows

        def include(current):
            key_block = lax.dynamic_slice_in_dim(span_key_rows, first_row, span_sub_rows, 0)
            value_block = lax.dynamic_slice_in_dim(span_value_rows, first_row, span_sub_rows, 0)
            key_position = first_row + jnp.arange(span_sub_rows, dtype=jnp.int32)
            live_mask = (key_position[None, :] <= query_position[:, None])[None]
            return online_update(current, key_block, value_block, live_mask)

        def skipped(current):
            return current

        return (lax.cond(first_row <= last_query, include, skipped, partial_value), None)

    span_running, _ = lax.scan(
        span_fold_step, span_running, jnp.arange(piece_rows // span_sub_rows, dtype=jnp.int32)
    )
    running = span_running
    peak_final, denominator, accumulated = running
    soft_out = (accumulated / denominator).astype(jnp.bfloat16)
    return (lightning_normalized_result, soft_out)


def solution(mesh):
    placed = (
        P("tp", "ctx", None),
        P("tp", "ctx", None),
        P("tp", "ctx", None),
        P("tp", "ctx"),
        P("tp", None, None),
        P("tp", None),
        P("tp", "ctx", None),
        P(None, "ctx", None),
        P(None, "ctx", None),
        P(None, "ctx", None),
        P(None, "ctx", None),
        P(),
    )
    return jax.shard_map(
        per_device,
        mesh=mesh,
        in_specs=placed,
        out_specs=(P("tp", "ctx", None), P("tp", "ctx", None)),
        check_vma=False,
    )
```

profile of v0, /device:TPU:408, one launch (start us, length us, event | category | flops | bytes accessed | tf_op | source)
XLA Modules:
  0.0 474.1 jit_solution(4882707199655224443)
XLA Ops:
  19.8 78.0 %all-reduce = bf16[128]{0:T(256)(128)(2,1)S(1)} all-reduce(bf16[128]{0:T(256)(128)(2,1)S(1)} %dynamic-update-slice), channel_id=2, replica_groups=mesh['ctx'=32,'tp'=16] {'ctx'}, use_global_device_ids=true, to_apply=%add | all-reduce | flops 128 | bytes 512
  99.4 48.9 %all-gather.16.cloned.1.call-done = bf16[1,4096,128]{2,1,0:T(8,128)(2,1)} async-done(((bf16[1,128,128]{2,1,0:T(8,128)(2,1)}), bf16[1,4096,128]{2,1,0:T(8,128)(2,1)}) %all-gather.16.cloned.1.call-update) | async-done | bytes 1048592 | tf_op jit(solution)/shard_map/all_gather | solution.py:168
  148.3 50.0 %while.53 = (s32[]{:T(128)}, f32[4,256,1]{1,0,2:T(4,128)S(1)}, f32[4,256,1]{1,0,2:T(4,128)S(1)}, f32[4,256,128]{2,1,0:T(8,128)}, s32[8]{0:T(128)S(1)}, /*index=5...) while((s32[]{:T(128)}, f32[4,256,1]{1,0,2:T(4,128)S(1)}, ...), condition=%wide.region_10.11_spmd.clone, body=%wide.region_6.10_spmd.clone.sunk | while | flops 275717120 | bytes 7940947 | solution.py:180
  198.3 25.8 %all-gather.18.cloned.1.call-done = bf16[1,8192,128]{2,1,0:T(8,128)(2,1)} async-done(((bf16[1,256,128]{2,1,0:T(8,128)(2,1)}), bf16[1,8192,128]{2,1,0:T(8,128)(2,1)}) %all-gather.18.cloned.1.call-update) | async-done | bytes 2097168 | tf_op jit(solution)/shard_map/all_gather | solution.py:184
  224.0 76.5 %all-gather.20.cloned.1.call-done = bf16[1,8192,128]{2,1,0:T(8,128)(2,1)} async-done(((bf16[1,256,128]{2,1,0:T(8,128)(2,1)}), bf16[1,8192,128]{2,1,0:T(8,128)(2,1)}) %all-gather.20.cloned.1.call-update) | async-done | bytes 2097168 | tf_op jit(solution)/shard_map/all_gather | solution.py:185
  300.5 88.9 %while.52 = (s32[]{:T(128)}, f32[4,256,1]{1,0,2:T(4,128)S(1)}, f32[4,256,1]{1,0,2:T(4,128)S(1)}, f32[4,256,128]{2,1,0:T(8,128)}, s32[16]{0:T(128)S(1)}, /*index=...) while((s32[]{:T(128)}, f32[4,256,1]{1,0,2:T(4,128)S(1)}, ...), condition=%wide.region_16.17_spmd.clone, body=%wide.region_11.16_spmd.clone.sunk | while | flops 275648256 | bytes 12657029 | solution.py:204
  301.8 4.3 conditional.3
  307.3 4.3 conditional.3
  312.9 4.3 conditional.3
  318.4 4.3 conditional.3
  324.0 4.3 conditional.3
  329.6 4.3 conditional.3
  335.1 4.3 conditional.3
  340.7 4.3 conditional.3
  346.2 4.3 conditional.3
  351.8 4.3 conditional.3
  357.3 4.3 conditional.3
  362.9 4.3 conditional.3
  368.4 4.3 conditional.3
  374.0 4.3 conditional.3
  379.6 4.3 conditional.3
  385.1 4.3 conditional.3
  393.7 32.1 %while.51 = (s32[]{:T(128)}, f32[4]{0:T(128)S(1)}, f32[4,128,128]{2,1,0:T(8,128)S(1)}, s32[]{:T(128)}, bf16[32,4]{1,0:T(8,128)(2,1)S(1)}, /*index=5*/bf16[32,4,1...) while((s32[]{:T(128)}, f32[4]{0:T(128)S(1)}, f32[4,128,128]{2,1,0:T(8,128)S(1)}, s32[]{:T(128)}, ...), condition=%wide.region_3.4_spmd, body=%wide.region_2.3_spmd.sunk | while | flops 196621 | bytes 655567 | solution.py:34
  426.9 39.6 %psum.7 = f32[256]{0:T(256)S(1)} all-reduce(f32[256]{0:T(256)S(1)} %get-tuple-element.420), channel_id=1, replica_groups=mesh['ctx'=32,'tp'=16] {'tp'}, use_global_device_ids=true, to_apply=%region_5.6 | all-reduce | flops 256 | bytes 2048 | tf_op jit(solution)/shard_map/psum | solution.py:117
  (446 shorter events, 172.1 us)
Async XLA Ops:
  7.2 3.0 copy-start
  7.2 141.1 %copy-start.1 = (bf16[4,256,128]{2,1,0:T(8,128)(2,1)S(1)}, bf16[4,256,128]{2,1,0:T(8,128)(2,1)}, u32[]{:S(2)}) copy-start(bf16[4,256,128]{2,1,0:T(8,128)(2,1)} %param.26) | copy-start | bytes 786436
  7.2 141.1 %copy-start.8 = (s32[32]{0:T(128)S(1)}, s32[32]{0:T(128)}, u32[]{:S(2)}) copy-start(s32[32]{0:T(128)} %param.31) | copy-start | bytes 388
  7.2 92.2 %all-gather.14.cloned.1.call-start = ((), (), s32[]{:S(2)}) async-start(), calls=%async_computation.1 | async-start | bytes 1081344 | tf_op jit(solution)/shard_map/all_gather | solution.py:167
  8.7 139.6 %all-gather.16.cloned.1.call-start = ((), (), s32[]{:S(2)}) async-start(), calls=%async_computation.2 | async-start | bytes 1081344 | tf_op jit(solution)/shard_map/all_gather | solution.py:168
  10.2 213.9 %all-gather.18.cloned.1.call-start = ((), (), s32[]{:S(2)}) async-start(), calls=%async_computation.3 | async-start | bytes 2162688 | tf_op jit(solution)/shard_map/all_gather | solution.py:184
  10.9 289.6 %all-gather.20.cloned.1.call-start = ((), (), s32[]{:S(2)}) async-start(), calls=%async_computation.4 | async-start | bytes 2162688 | tf_op jit(solution)/shard_map/all_gather | solution.py:185
  12.4 381.2 %all-gather.12.cloned.1.call-start = ((), (), s32[]{:S(2)}) async-start(), calls=%async_computation | async-start | bytes 4325376 | tf_op jit(solution)/shard_map/all_gather | solution.py:20
  301.8 1.6 copy-start.3
  307.4 1.6 copy-start.3
  318.5 1.6 copy-start.3
  324.0 1.6 copy-start.3
  329.6 1.6 copy-start.3
  335.1 1.6 copy-start.3
  340.7 1.6 copy-start.3
  346.2 1.6 copy-start.3
  351.8 1.6 copy-start.3
  374.0 1.6 copy-start.3
  379.6 1.6 copy-start.3
  389.4 36.4 %copy-start.2 = (bf16[4,256,128]{2,1,0:T(8,128)(2,1)S(1)}, bf16[4,256,128]{2,1,0:T(8,128)(2,1)}, u32[]{:S(2)}) copy-start(bf16[4,256,128]{2,1,0:T(8,128)(2,1)} %param.20) | copy-start | bytes 786436
  389.4 36.4 %copy-start.5 = (f32[4,128,128]{2,1,0:T(8,128)S(1)}, f32[4,128,128]{2,1,0:T(8,128)}, u32[]{:S(2)}) copy-start(f32[4,128,128]{2,1,0:T(8,128)} %param.24) | copy-start | bytes 786436
  393.7 32.6 %copy-start.6 = (bf16[4,256,128]{2,1,0:T(8,128)(2,1)S(1)}, bf16[4,256,128]{2,1,0:T(8,128)(2,1)}, u32[]{:S(2)}) copy-start(bf16[4,256,128]{2,1,0:T(8,128)(2,1)} %param.22) | copy-start | bytes 786436
  393.7 32.6 %copy-start.7 = (bf16[4,256,128]{2,1,0:T(8,128)(2,1)S(1)}, bf16[4,256,128]{2,1,0:T(8,128)(2,1)}, u32[]{:S(2)}) copy-start(bf16[4,256,128]{2,1,0:T(8,128)(2,1)} %param.21) | copy-start | bytes 786436
  425.8 40.7 %copy-start.9 = (f32[4,128]{1,0:T(4,128)S(1)}, f32[4,128]{1,0:T(4,128)}, u32[]{:S(2)}) copy-start(f32[4,128]{1,0:T(4,128)} %param.25) | copy-start | bytes 6148
  (21 other events, 21.2 us)
Sparse Core Ops, SparseCore 0:
  11.2 69.0 all-gather.13
  83.4 64.8 all-gather.15
  152.0 71.9 all-gather.17
  227.0 73.4 all-gather.19
  304.1 89.5 all-gather.11
where the time goes:
time: 476 us; the launch traced here: 474 us
  waiting for transfers between devices  154 us (32%)
  blocking collectives  118 us (25%)
  matrix products  90.3 us (19%)
  other arithmetic  52.1 us (11%)
  local copies, waits for them, and re-layouts  27.1 us (6%)
  loops' own time  18.5 us (4%)
  between operations  14.7 us (3%)
    unnamed x1, blocking collectives  78 us
    all_gather x1, waiting for transfers between devices, per_device(): span_value_rows = lax.all_gather(head_values, 'ctx', axis=0, tiled=True)  76.5 us
    dot_general x24, matrix products, online_update(): jnp.einsum('hqk,kd->hqd', probabilities.astype(jnp.bfloat16), value_block...  51.9 us
    all_gather x1, waiting for transfers between devices, per_device(): value_rows = lax.all_gather(cache_head_values, 'ctx', axis=0, tiled=True)  48.9 us
    psum x1, blocking collectives, per_device(): total_squares = lax.psum(square_sums, 'tp')  39.6 us
    dot_general x24, matrix products, online_update(): jnp.einsum('hqd,kd->hqk', soft_q, key_block, preferred_element_type=jnp.f...  33.6 us
    add x30, other arithmetic, combine(): jnp.exp(latter[0])[:, None, None] * earlier[1] + latter[1]  30.6 us
    all_gather x1, waiting for transfers between devices, per_device(): span_key_rows = lax.all_gather(head_keys, 'ctx', axis=0, tiled=True)  25.8 us
  transfers between devices with their start and end apart: 5, of which 4 were waited for; matrix products, arithmetic and copies ran while one was open for 28% of the time, Pallas kernels for 0%

commit v1 on v0

v1 whole, which is shorter than its diff:
```python
import functools
import math

import jax
import jax.numpy as jnp
from jax import lax
from jax.experimental import pallas as pl
from jax.experimental.pallas import tpu as pltpu
from jax.sharding import PartitionSpec as P

GROUP_Q = 8
N_Z, N_Y, N_CORE = 4, 4, 2
N_CTX = N_Z * N_Y * N_CORE
N_YC = N_Y * N_CORE
HD = 128
HEADS_DEV = 4
TOK = 256
CROWS = 128
PAY = 2 * TOK + 2 * CROWS
KCHUNK = 1024
MASK_FILL = -1e30
LOG2E = 1.4426950408889634
VMEM_LIMIT = 48 * 1024 * 1024

F32 = jnp.float32
BF16 = jnp.bfloat16

Z_GROUPS = [[z * N_YC + r for z in range(N_Z)] for r in range(N_YC)]
YC_GROUPS = [[z * N_YC + r for r in range(N_YC)] for z in range(N_Z)]

NT = (((1,), (1,)), ((), ()))
NN = (((1,), (0,)), ((), ()))
TN = (((0,), (0,)), ((), ()))


def dot(a, b, dims):
    return lax.dot_general(a, b, dims, preferred_element_type=F32)


def split3(x):
    hi = x.astype(BF16)
    rest = x - hi.astype(F32)
    mid = rest.astype(BF16)
    low = (rest - mid.astype(F32)).astype(BF16)
    return hi, mid, low


def split2(x):
    hi = x.astype(BF16)
    return hi, (x - hi.astype(F32)).astype(BF16)


def pack_kernel(head_ref, sk_ref, sv_ref, ck_ref, cv_ref, out_ref):
    out_ref[0:TOK, :] = sk_ref[0]
    out_ref[TOK : 2 * TOK, :] = sv_ref[0]
    out_ref[2 * TOK : 2 * TOK + CROWS, :] = ck_ref[0]
    out_ref[2 * TOK + CROWS : PAY, :] = cv_ref[0]


def pack(kv_head, span_k, span_v, cache_k, cache_v):
    def spec(rows):
        return pl.BlockSpec((1, rows, HD), lambda i, h: (h[0], 0, 0))

    return pl.pallas_call(
        pack_kernel,
        out_shape=jax.ShapeDtypeStruct((PAY, HD), BF16),
        grid_spec=pltpu.PrefetchScalarGridSpec(
            num_scalar_prefetch=1,
            grid=(1,),
            in_specs=[spec(TOK), spec(TOK), spec(CROWS), spec(CROWS)],
            out_specs=pl.BlockSpec((PAY, HD), lambda i, h: (0, 0)),
        ),
        name="pack_kv",
    )(kv_head, span_k, span_v, cache_k, cache_v)


def lightning_local_kernel(place_ref, q_ref, k_ref, v_ref, decay_ref, prior_ref, mixed_ref, cum_ref, pay_ref):
    first = jnp.where(place_ref[0] == 0, 1.0, 0.0).astype(F32)
    t_ids = lax.broadcasted_iota(jnp.int32, (TOK, TOK), 0)
    s_ids = lax.broadcasted_iota(jnp.int32, (TOK, TOK), 1)
    lower = t_ids >= s_ids
    tri = jnp.where(lower, 1.0, 0.0).astype(BF16)
    parts = split3(jnp.concatenate([decay_ref[...], decay_ref[...]], axis=0))
    cum_rows = sum(dot(p, tri, NT) for p in parts)
    cum_cols = sum(dot(tri, p, NT) for p in parts)
    cum_ref[...] = cum_cols
    pieces = HD // 16
    for h in range(HEADS_DEV):
        row = cum_rows[h : h + 1, :]
        col = cum_cols[:, h : h + 1]
        final = cum_rows[h : h + 1, TOK - 1 : TOK]
        q, k, v = q_ref[h], k_ref[h], v_ref[h]
        gap = jnp.where(lower, col - row, 0.0)
        weights = jnp.where(lower, dot(q, k, NT) * jnp.exp(gap), 0.0).astype(BF16)
        mixed_ref[h] = dot(weights, v, NN)
        keyed_hi, keyed_lo = split2(k.astype(F32) * jnp.exp(final - col))
        state = dot(keyed_hi, v, TN) + dot(keyed_lo, v, TN)
        state = state + (first * jnp.exp(final)) * prior_ref[h]
        pay_ref[h * pieces : (h + 1) * pieces, 0:16, :] = state.astype(BF16).reshape(pieces, 16, HD)
        line = jnp.broadcast_to(final, (16, HD))
        d_hi, d_mid, d_low = (p.astype(F32) for p in split3(line))
        ids = lax.broadcasted_iota(jnp.int32, (16, HD), 0)
        block = jnp.where(ids == 0, d_hi, jnp.where(ids == 1, d_mid, d_low)).astype(BF16)
        for i in range(pieces):
            pay_ref[h * pieces + i, 16:32, :] = block


def lightning_local(place, lin_q, lin_k, lin_v, log_decay, prior_state):
    vmem = pl.BlockSpec(memory_space=pltpu.VMEM)
    return pl.pallas_call(
        lightning_local_kernel,
        out_shape=(
            jax.ShapeDtypeStruct((HEADS_DEV, TOK, HD), F32),
            jax.ShapeDtypeStruct((TOK, 2 * HEADS_DEV), F32),
            jax.ShapeDtypeStruct((N_CTX, 32, HD), BF16),
        ),
        in_specs=[pl.BlockSpec(memory_space=pltpu.SMEM)] + [vmem] * 5,
        out_specs=(vmem, vmem, vmem),
        compiler_params=pltpu.CompilerParams(vmem_limit_bytes=VMEM_LIMIT),
        name="lightning_local",
    )(place, lin_q, lin_k, lin_v, log_decay, prior_state)


def scan_kernel(in_ref, out_ref):
    acc = jnp.zeros((16, HD), F32)
    for c in range(N_CTX):
        out_ref[c] = acc.astype(BF16)
        if c + 1 < N_CTX:
            tail = in_ref[c, 16:32, :].astype(F32)
            decay = tail[0:1] + tail[1:2] + tail[2:3]
            acc = acc * jnp.exp(decay) + in_ref[c, 0:16, :].astype(F32)


def scan_pieces(pieces):
    vmem = pl.BlockSpec(memory_space=pltpu.VMEM)
    return pl.pallas_call(
        scan_kernel,
        out_shape=jax.ShapeDtypeStruct((N_CTX, 16, HD), BF16),
        in_specs=[vmem],
        out_specs=vmem,
        name="scan_states",
    )(pieces)


def lightning_mix_kernel(place_ref, q_ref, mixed_ref, cum_ref, carried_ref, prior_ref, out_ref, square_ref):
    first = place_ref[0] == 0
    total = jnp.zeros((TOK, HD), F32)
    for h in range(HEADS_DEV):
        state = jnp.where(first, prior_ref[h], carried_ref[h].astype(F32))
        hi, low = split2(state)
        q = q_ref[h]
        inter = dot(q, hi, NN) + dot(q, low, NN)
        mixed = mixed_ref[h] + jnp.exp(cum_ref[:, h : h + 1]) * inter
        out_ref[h] = mixed
        total = total + mixed * mixed
    ones = jnp.ones((8, HD), BF16)
    square_ref[...] = sum(dot(ones, p, NT) for p in split3(total))


def lightning_mix(place, lin_q, mixed, cum, carried, prior_state):
    vmem = pl.BlockSpec(memory_space=pltpu.VMEM)
    return pl.pallas_call(
        lightning_mix_kernel,
        out_shape=(
            jax.ShapeDtypeStruct((HEADS_DEV, TOK, HD), F32),
            jax.ShapeDtypeStruct((8, TOK), F32),
        ),
        in_specs=[pl.BlockSpec(memory_space=pltpu.SMEM)] + [vmem] * 5,
        out_specs=(vmem, vmem),
        compiler_params=pltpu.CompilerParams(vmem_limit_bytes=VMEM_LIMIT),
        name="lightning_mix",
    )(place, lin_q, mixed, cum, carried, prior_state)


def norm_kernel(count, mixed_ref, squares_ref, gain_ref, out_ref):
    total = jnp.sum(squares_ref[...], axis=0)
    inv = lax.rsqrt(total * (1.0 / count) + 1e-05)
    t_ids = lax.broadcasted_iota(jnp.int32, (HD, HD), 0)
    s_ids = lax.broadcasted_iota(jnp.int32, (HD, HD), 1)
    for half in range(TOK // HD):
        diag = jnp.where(t_ids == s_ids, jnp.broadcast_to(inv[half : half + 1, :], (HD, HD)), 0.0)
        col = jnp.sum(diag, axis=1, keepdims=True)
        rows = slice(half * HD, (half + 1) * HD)
        for h in range(HEADS_DEV):
            out_ref[h, rows, :] = (mixed_ref[h, rows, :] * col * gain_ref[h : h + 1, :]).astype(BF16)


def lightning_norm(count, mixed, squares, gain):
    vmem = pl.BlockSpec(memory_space=pltpu.VMEM)
    return pl.pallas_call(
        functools.partial(norm_kernel, float(count)),
        out_shape=jax.ShapeDtypeStruct((HEADS_DEV, TOK, HD), BF16),
        in_specs=[vmem] * 3,
        out_specs=vmem,
        compiler_params=pltpu.CompilerParams(vmem_limit_bytes=VMEM_LIMIT),
        name="lightning_norm",
    )(mixed, squares, gain)


def attention_kernel(scale, info_ref, q_ref, kv_hbm, out_ref, ckv, skv, qs, m_ref, l_ref, acc_ref, csem, ssem):
    place = info_ref[N_CTX]
    last_chunk = place // 4
    n_cache = N_CTX * CROWS // KCHUNK
    yc_step = N_YC // n_cache

    def cache_copy(i):
        return pltpu.make_async_copy(
            kv_hbm.at[pl.ds(i * yc_step, yc_step), :, pl.ds(2 * TOK, 2 * CROWS), :], ckv.at[i], csem.at[i]
        )

    def span_copy(j):
        return pltpu.make_async_copy(
            kv_hbm.at[pl.ds((j % 2) * 4, 4), j // 2, pl.ds(0, 2 * TOK), :], skv.at[j], ssem.at[j]
        )

    for i in range(n_cache):
        cache_copy(i).start()

    def start(j, _):
        span_copy(j).start()
        return 0

    lax.fori_loop(0, last_chunk + 1, start, 0)

    for h in range(HEADS_DEV):
        hi, low = split2(q_ref[h].astype(F32) * scale)
        qs[h, :, 0:HD] = hi
        qs[h, :, HD : 2 * HD] = low
    m_ref[...] = jnp.full_like(m_ref, MASK_FILL)
    l_ref[...] = jnp.zeros_like(l_ref)
    acc_ref[...] = jnp.zeros_like(acc_ref)

    def update(keys, values, mask):
        wide = jnp.concatenate([keys, keys], axis=1)
        for h in range(HEADS_DEV):
            scores = mask(dot(qs[h], wide, NT))
            m_old = m_ref[h]
            m_new = jnp.maximum(m_old, jnp.max(scores, axis=1, keepdims=True))
            probs = jnp.exp2(scores - m_new[:, 0:1])
            alpha = jnp.exp2(m_old - m_new)
            m_ref[h] = m_new
            l_ref[h] = l_ref[h] * alpha + jnp.sum(probs, axis=1, keepdims=True)
            acc_ref[h] = acc_ref[h] * alpha + dot(probs.astype(BF16), values, NN)

    lanes = lax.broadcasted_iota(jnp.int32, (1, CROWS), 1)

    for i in range(n_cache):
        cache_copy(i).wait()
        bias = []
        for r in range(yc_step):
            for z in range(N_Z):
                live = info_ref[z * N_YC + i * yc_step + r]
                bias.append(jnp.where(lanes < live, 0.0, MASK_FILL).astype(F32))
        bias = jnp.concatenate(bias, axis=1)
        block = ckv[i].reshape(yc_step * N_Z, 2, CROWS, HD)
        update(
            block[:, 0].reshape(KCHUNK, HD), block[:, 1].reshape(KCHUNK, HD), lambda s: s + bias
        )

    def span_kv(j):
        span_copy(j).wait()
        block = skv[j].reshape(4, 2, TOK, HD)
        return block[:, 0].reshape(KCHUNK, HD), block[:, 1].reshape(KCHUNK, HD)

    def full(j, _):
        keys, values = span_kv(j)
        update(keys, values, lambda s: s)
        return 0

    lax.fori_loop(0, last_chunk, full, 0)
    keys, values = span_kv(last_chunk)
    offset = (place - last_chunk * 4) * TOK
    rows = lax.broadcasted_iota(jnp.int32, (TOK, KCHUNK), 0) + offset
    cols = lax.broadcasted_iota(jnp.int32, (TOK, KCHUNK), 1)
    update(keys, values, lambda s: jnp.where(cols <= rows, s, MASK_FILL))
    for h in range(HEADS_DEV):
        out_ref[h] = (acc_ref[h] / l_ref[h]).astype(BF16)


def attention(info, soft_q, kv):
    vmem = pl.BlockSpec(memory_space=pltpu.VMEM)
    n_cache = N_CTX * CROWS // KCHUNK
    n_span = N_CTX * TOK // KCHUNK
    stat = pltpu.VMEM((HEADS_DEV, TOK, HD), F32)
    return pl.pallas_call(
        functools.partial(attention_kernel, LOG2E / math.sqrt(HD)),
        out_shape=jax.ShapeDtypeStruct((HEADS_DEV, TOK, HD), BF16),
        in_specs=[pl.BlockSpec(memory_space=pltpu.SMEM), vmem, pl.BlockSpec(memory_space=pl.ANY)],
        out_specs=vmem,
        scratch_shapes=[
            pltpu.VMEM((n_cache, N_YC // n_cache, N_Z, 2 * CROWS, HD), BF16),
            pltpu.VMEM((n_span, 4, 2 * TOK, HD), BF16),
            pltpu.VMEM((HEADS_DEV, TOK, 2 * HD), BF16),
            stat,
            stat,
            stat,
            pltpu.SemaphoreType.DMA((n_cache,)),
            pltpu.SemaphoreType.DMA((n_span,)),
        ],
        compiler_params=pltpu.CompilerParams(vmem_limit_bytes=VMEM_LIMIT),
        name="softmax_attention",
    )(info, soft_q, kv)


def per_device(
    lin_q,
    lin_k,
    lin_v,
    log_decay,
    prior_state,
    lin_gain,
    soft_q,
    span_k,
    span_v,
    cache_k,
    cached_value_rows,
    cache_len,
):
    ctx = lax.axis_index("ctx").astype(jnp.int32)
    tp = lax.axis_index("tp").astype(jnp.int32)
    place = ctx.reshape(1)
    kv_head = (tp * HEADS_DEV // GROUP_Q).reshape(1)

    payload = pack(kv_head, span_k, span_v, cache_k, cached_value_rows)
    column = lax.all_gather(payload, "ctx", axis=0, tiled=True, axis_index_groups=Z_GROUPS)
    kv = lax.all_gather(column, "ctx", axis=0, tiled=True, axis_index_groups=YC_GROUPS)
    kv = kv.reshape(N_YC, N_Z, PAY, HD)

    mixed, cum, pay = lightning_local(place, lin_q, lin_k, lin_v, log_decay, prior_state)
    pieces = lax.all_to_all(pay, "ctx", 0, 0)
    prefixes = scan_pieces(pieces)
    carried = lax.all_to_all(prefixes, "ctx", 0, 0).reshape(HEADS_DEV, HD, HD)
    mixed, squares = lightning_mix(place, lin_q, mixed, cum, carried, prior_state)
    n_tp = lax.axis_size("tp")
    own = squares[0].reshape(1, TOK // HD, HD)
    all_squares = lax.all_to_all(jnp.broadcast_to(own, (n_tp, TOK // HD, HD)), "tp", 0, 0)
    normalized = lightning_norm(n_tp * HEADS_DEV * HD, mixed, all_squares, lin_gain)

    info = jnp.concatenate([cache_len, place])
    soft_out = attention(info, soft_q, kv)
    return (normalized, soft_out)


def solution(mesh):
    placed = (
        P("tp", "ctx", None),
        P("tp", "ctx", None),
        P("tp", "ctx", None),
        P("tp", "ctx"),
        P("tp", None, None),
        P("tp", None),
        P("tp", "ctx", None),
        P(None, "ctx", None),
        P(None, "ctx", None),
        P(None, "ctx", None),
        P(None, "ctx", None),
        P(),
    )
    return jax.shard_map(
        per_device,
        mesh=mesh,
        in_specs=placed,
        out_specs=(P("tp", "ctx", None), P("tp", "ctx", None)),
        check_vma=False,
    )
```

time: 476 us -> 158 us (0.33)
  waiting for transfers between devices: 154 us -> 7.93 us
  matrix products: 90.3 us -> 0 us
  other arithmetic: 52.1 us -> 0.08 us
  Pallas kernels: 0 us -> 38.8 us
  blocking collectives: 118 us -> 83.5 us
  local copies, waits for them, and re-layouts: 27.1 us -> 7.04 us
  loops' own time: 18.5 us -> 0 us
  starting transfers between devices: 0.21 us -> 5.51 us
    all_gather x5 -> x1, waiting for transfers between devices: 153 us -> 0.01 us  [per_device(): lax.all_gather(column, 'ctx', axis=0, tiled=True, axis_index_groups=YC_GR...]
    dot_general x52 -> x0, matrix products: 90.3 us -> none  [the longest x24 51.9 us: online_update(): jnp.einsum('hqk,kd->hqd', probabilities.astype(jnp.bfloat16), value_block...]
    unnamed x1 -> x0, blocking collectives: 78 us -> none
    all_to_all x0 -> x2, blocking collectives: none -> 49.8 us  [the longest x1 25.6 us: per_device(): pieces = lax.all_to_all(pay, 'ctx', 0, 0)]
    psum x1 -> x0, blocking collectives: 39.6 us -> none  [per_device(): total_squares = lax.psum(square_sums, 'tp')]
    pallas_call x0 -> x6, Pallas kernels: none -> 38.8 us  [the longest x1 32.7 us: attention(): pl.pallas_call(functools.partial(attention_kernel, LOG2E / math.sqrt(HD))...]
    all_gather x0 -> x1, blocking collectives: none -> 33.7 us  [per_device(): lax.all_gather(payload, 'ctx', axis=0, tiled=True, axis_index_groups=Z_GR...]
    add x86 -> x0, other arithmetic: 31.2 us -> none  [the longest x30 30.6 us: combine(): jnp.exp(latter[0])[:, None, None] * earlier[1] + latter[1]]
  transfers between devices with their start and end apart: 5 -> 2, of which waited for: 4 -> 1; matrix products, arithmetic and copies ran while one was open for 28% -> 0% of each run, Pallas kernels for 0% -> 3%
where the time goes in v1:
time: 158 us; the launch traced here: 157 us
  blocking collectives  83.5 us (53%)
  Pallas kernels  38.8 us (25%)
  between operations  14.1 us (9%)
  waiting for transfers between devices  7.93 us (5%)
  local copies, waits for them, and re-layouts  7.04 us (4%)
  starting transfers between devices  5.51 us (3%)
    all_gather x1, blocking collectives, per_device(): lax.all_gather(payload, 'ctx', axis=0, tiled=True, axis_index_groups=Z_GR...  33.7 us
    pallas_call x1, Pallas kernels, attention(): pl.pallas_call(functools.partial(attention_kernel, LOG2E / math.sqrt(HD))...  32.7 us
    all_to_all x1, blocking collectives, per_device(): pieces = lax.all_to_all(pay, 'ctx', 0, 0)  25.6 us
    all_to_all x1, blocking collectives, per_device(): carried = lax.all_to_all(prefixes, 'ctx', 0, 0).reshape(HEADS_DEV, HD, HD)  24.2 us
    all_to_all x1, waiting for transfers between devices, per_device(): lax.all_to_all(jnp.broadcast_to(own, (n_tp, TOK // HD, HD)), 'tp', 0, 0)  7.91 us
    unnamed x20, local copies, waits for them, and re-layouts  6.39 us
    all_to_all x1, starting transfers between devices, per_device(): lax.all_to_all(jnp.broadcast_to(own, (n_tp, TOK // HD, HD)), 'tp', 0, 0)  5.48 us
  transfers between devices with their start and end apart: 2, of which 1 were waited for; matrix products, arithmetic and copies ran while one was open for 0% of the time, Pallas kernels for 3%

profile of v1, /device:TPU:408, one launch (start us, length us, event | category | flops | bytes accessed | tf_op | source)
XLA Modules:
  0.0 157.0 jit_solution(4979177843922756655)
XLA Ops:
  7.2 0.0 copy-start.9
  7.2 0.0 all-gather.2.cloned.1.call-start
  7.3 1.6 %pack_kv.1 = bf16[768,128]{1,0:T(8,128)(2,1)} custom-call(s32[1]{0:T(128)} %bitcast.3.head_ref, bf16[8,256,128]{2,1,0:T(8,128)(2,1)} %sk_ref.1, bf16[8,256,128]{2,1,0:T(8,128)(2,1)} %sv_ref.1, bf16[8,128,128]{2,1,0:T(8,128)(2,1)} %ck_ref.1, bf16[8,128,128]{2,1,0:T(8,128)(2,1)} %cv_ref.1), custom_call_target="tpu_custom_call" | custom-call | tf_op jit(solution)/shard_map/pack_kv/pallas_call | solution.py:64
  8.9 33.7 %all_gather.6 = bf16[3072,128]{1,0:T(8,128)(2,1)} all-gather(bf16[768,128]{1,0:T(8,128)(2,1)} %pack_kv.1), channel_id=1, replica_groups={{0,128,256,384},{16,144,272,400},{32,160,288,416},{48,176,304,432},{64,..., dimensions={0}, use_global_device_ids=true | all-gather | bytes 983040 | tf_op jit(solution)/shard_map/all_gather | solution.py:325
  42.6 0.0 all-gather.2.cloned.1.call-update
  42.6 0.0 copy-start
  42.6 0.9 copy-done
  43.5 0.9 copy-done.2
  44.5 0.9 copy-done.5
  45.4 0.9 copy-done.6
  46.4 0.7 copy-done.7
  47.1 1.5 lightning_local.1
  48.6 25.6 %all_to_all.15.in_ref = bf16[32,32,128]{2,1,0:T(8,128)(2,1)} all-to-all(bf16[32,32,128]{2,1,0:T(8,128)(2,1)S(1)} %get-tuple-element.9), channel_id=1, replica_groups=mesh['ctx'=32,'tp'=16] {'ctx'}, dimensions={0} | all-to-all | bytes 524288 | tf_op jit(solution)/shard_map/all_to_all | solution.py:330
  74.1 1.7 %scan_states.1 = bf16[32,16,128]{2,1,0:T(8,128)(2,1)} custom-call(bf16[32,32,128]{2,1,0:T(8,128)(2,1)} %all_to_all.15.in_ref), custom_call_target="tpu_custom_call" | custom-call | tf_op jit(solution)/shard_map/scan_states/pallas_call | solution.py:136
  75.8 24.2 %all_to_all.16 = bf16[32,16,128]{2,1,0:T(8,128)(2,1)S(1)} all-to-all(bf16[32,16,128]{2,1,0:T(8,128)(2,1)} %scan_states.1), channel_id=1, replica_groups=mesh['ctx'=32,'tp'=16] {'ctx'}, dimensions={0} | all-to-all | bytes 262144 | tf_op jit(solution)/shard_map/all_to_all | solution.py:332
  100.0 0.9 copy-done.1
  101.0 0.9 copy-done.3
  101.9 0.5 lightning_mix.1
  102.4 0.6 broadcast_in_dim.8
  103.1 5.5 %all-to-all-start.2 = ((f32[16,2,128]{2,1,0:T(2,128)}), f32[16,2,128]{2,1,0:T(2,128)S(1)}, u32[]{:S(2)}, u32[]{:S(2)}) async-start(f32[16,2,128]{2,1,0:T(2,128)} %broadcast_in_dim.8), calls=%async_computation.2 | async-start | bytes 32768 | tf_op jit(solution)/shard_map/all_to_all | solution.py:336
  108.6 0.1 pad_add_fusion.info_ref
  108.6 7.9 %all-to-all-done.2.squares_ref = f32[16,2,128]{2,1,0:T(2,128)S(1)} async-done(((f32[16,2,128]{2,1,0:T(2,128)}), f32[16,2,128]{2,1,0:T(2,128)S(1)}, u32[]{:S(2)}, u32[]{:S(2)}) %all-to-all-start.2) | async-done | bytes 16416 | tf_op jit(solution)/shard_map/all_to_all | solution.py:336
  116.6 0.9 lightning_norm.1
  117.4 32.7 %softmax_attention.1 = bf16[4,256,128]{2,1,0:T(8,128)(2,1)} custom-call(s32[33]{0:T(128)S(1)} %pad_add_fusion.info_ref, bf16[4,256,128]{2,1,0:T(8,128)(2,1)S(1)} %copy-done.4, bf16[8,4,768,128]{3,2,1,0:T(8,128)(2,1)} %bitcast.6), custom_call_target="tpu_custom_call" | custom-call | tf_op jit(solution)/shard_map/softmax_attention/pallas_call | solution.py:285
  (13 shorter events, 0.0 us)
Async XLA Ops:
  7.2 101.4 %copy-start.9 = (s32[32]{0:T(128)S(1)}, s32[32]{0:T(128)}, u32[]{:S(2)}) copy-start(s32[32]{0:T(128)} %param.23) | copy-start | bytes 388
  7.2 109.4 %copy-start.8 = (f32[4,128]{1,0:T(4,128)S(1)}, f32[4,128]{1,0:T(4,128)}, u32[]{:S(2)}) copy-start(f32[4,128]{1,0:T(4,128)} %gain_ref.1) | copy-start | bytes 6148
  7.2 110.2 %copy-start.4 = (bf16[4,256,128]{2,1,0:T(8,128)(2,1)S(1)}, bf16[4,256,128]{2,1,0:T(8,128)(2,1)}, u32[]{:S(2)}) copy-start(bf16[4,256,128]{2,1,0:T(8,128)(2,1)} %q_ref.5) | copy-start | bytes 786436
  7.2 110.2 %all-gather.2.cloned.1.call-start = ((), (), s32[]{:S(2)}) async-start(), calls=%async_computation.3 | async-start | bytes 7077888 | tf_op jit(solution)/shard_map/all_gather | solution.py:326
  42.6 1.0 copy-start
  43.5 0.9 copy-start.2
  44.5 0.9 copy-start.5
  45.4 0.9 copy-start.6
  46.4 0.7 copy-start.7
  100.0 1.0 copy-start.1
  101.0 0.9 copy-start.3
  103.1 13.5 %all-to-all-start.2 = ((f32[16,2,128]{2,1,0:T(2,128)}), f32[16,2,128]{2,1,0:T(2,128)S(1)}, u32[]{:S(2)}, u32[]{:S(2)}) async-start(f32[16,2,128]{2,1,0:T(2,128)} %broadcast_in_dim.8), calls=%async_computation.2 | async-start | bytes 32768 | tf_op jit(solution)/shard_map/all_to_all | solution.py:336
Sparse Core Ops, SparseCore 0:
  42.7 50.4 all-gather.1

commit v2 on v1

v2 whole, which is shorter than its diff:
```python
import functools
import math

import jax
import jax.numpy as jnp
from jax import lax
from jax.experimental import pallas as pl
from jax.experimental.pallas import tpu as pltpu
from jax.sharding import PartitionSpec as P

GROUP_Q = 8
N_Z, N_Y, N_CORE = 4, 4, 2
N_CTX = N_Z * N_Y * N_CORE
N_YC = N_Y * N_CORE
HD = 128
HEADS_DEV = 4
TOK = 256
CROWS = 128
KROWS = TOK + CROWS
PAY = 2 * KROWS
D_ROWS = 16
S_ROWS = HEADS_DEV * HD + D_ROWS
HEADS_CORE = HEADS_DEV // N_CORE
U_ROWS = HEADS_CORE * HD + D_ROWS
MASK_FILL = -1e30
LOG2E = 1.4426950408889634
VMEM_LIMIT = 60 * 1024 * 1024

F32 = jnp.float32
BF16 = jnp.bfloat16

Z_GROUPS = [[z * N_YC + r for z in range(N_Z)] for r in range(N_YC)]
YC_GROUPS = [[z * N_YC + r for r in range(N_YC)] for z in range(N_Z)]
CORE_GROUPS = [[N_CORE * r + i for i in range(N_CORE)] for r in range(N_CTX // N_CORE)]

NT = (((1,), (1,)), ((), ()))
NN = (((1,), (0,)), ((), ()))
TN = (((0,), (0,)), ((), ()))


def dot(a, b, dims):
    return lax.dot_general(a, b, dims, preferred_element_type=F32)


def split3(x):
    hi = x.astype(BF16)
    rest = x - hi.astype(F32)
    mid = rest.astype(BF16)
    low = (rest - mid.astype(F32)).astype(BF16)
    return hi, mid, low


def split2(x):
    hi = x.astype(BF16)
    return hi, (x - hi.astype(F32)).astype(BF16)


HBM = pl.BlockSpec(memory_space=pltpu.HBM)
VMEM = pl.BlockSpec(memory_space=pltpu.VMEM)
SMEM = pl.BlockSpec(memory_space=pltpu.SMEM)
LIN = (HEADS_DEV, TOK, HD)
STATE = (HEADS_DEV, HD, HD)


def begin(pairs, sems, base=0):
    copies = [pltpu.make_async_copy(a, b, sems.at[base + i]) for i, (a, b) in enumerate(pairs)]
    for copy in copies:
        copy.start()
    return copies


def finish(copies):
    for copy in copies:
        copy.wait()


def run(kernel, name, operands, in_specs, outs, scratch, n_sems):
    single = len(outs) == 1
    shapes = tuple(jax.ShapeDtypeStruct(shape, kind) for shape, kind, _ in outs)
    specs = tuple(spec for _, _, spec in outs)
    return pl.pallas_call(
        kernel,
        out_shape=shapes[0] if single else shapes,
        in_specs=in_specs,
        out_specs=specs[0] if single else specs,
        scratch_shapes=[pltpu.VMEM(shape, kind) for shape, kind in scratch]
        + [pltpu.SemaphoreType.DMA((n_sems,))],
        compiler_params=pltpu.CompilerParams(vmem_limit_bytes=VMEM_LIMIT),
        name=name,
    )(*operands)


def decay_lines(values):
    ids = lax.broadcasted_iota(jnp.int32, (D_ROWS, HD), 0)
    lines = jnp.zeros((D_ROWS, HD), F32)
    for h, value in enumerate(values):
        for i, part in enumerate(split3(jnp.broadcast_to(value, (1, HD)))):
            lines = jnp.where(ids == 3 * h + i, part.astype(F32), lines)
    return lines.astype(BF16)


def decay_of(lines, h):
    lines = lines[3 * h : 3 * h + 3].astype(F32)
    return lines[0:1] + lines[1:2] + lines[2:3]


def prep_kernel(
    info_ref, sk_hbm, sv_hbm, ck_hbm, cv_hbm, q_hbm, k_hbm, v_hbm, decay_hbm, prior_hbm,
    payload_hbm, plane_hbm, mixed_hbm, cum_hbm,
    kv_ref, q_ref, k_ref, v_ref, decay_ref, prior_ref, mixed_ref, cum_ref, state_ref, sems,
):
    head = info_ref[0]
    packs = begin(
        [
            (sk_hbm.at[head], kv_ref.at[pl.ds(0, TOK), :]),
            (ck_hbm.at[head], kv_ref.at[pl.ds(TOK, CROWS), :]),
            (sv_hbm.at[head], kv_ref.at[pl.ds(KROWS, TOK), :]),
            (cv_hbm.at[head], kv_ref.at[pl.ds(KROWS + TOK, CROWS), :]),
        ],
        sems,
    )
    loads = begin(
        [(decay_hbm, decay_ref), (q_hbm, q_ref), (k_hbm, k_ref), (v_hbm, v_ref), (prior_hbm, prior_ref)],
        sems,
        4,
    )
    finish(packs)
    packs = begin([(kv_ref, payload_hbm), (kv_ref, plane_hbm.at[pl.ds(0, PAY), :])], sems, 9)
    finish(loads)
    first = jnp.where(info_ref[1] == 0, 1.0, 0.0).astype(F32)
    t_ids = lax.broadcasted_iota(jnp.int32, (TOK, TOK), 0)
    s_ids = lax.broadcasted_iota(jnp.int32, (TOK, TOK), 1)
    lower = t_ids >= s_ids
    tri = jnp.where(lower, 1.0, 0.0).astype(BF16)
    parts = split3(jnp.concatenate([decay_ref[...], decay_ref[...]], axis=0))
    cum_rows = sum(dot(p, tri, NT) for p in parts)
    cum_cols = sum(dot(tri, p, NT) for p in parts)
    cum_ref[...] = cum_cols
    finals = []
    for h in range(HEADS_DEV):
        row = cum_rows[h : h + 1, :]
        col = cum_cols[:, h : h + 1]
        final = cum_rows[h : h + 1, TOK - 1 : TOK]
        finals.append(final)
        q, k, v = q_ref[h], k_ref[h], v_ref[h]
        gap = jnp.where(lower, col - row, 0.0)
        weights = jnp.where(lower, dot(q, k, NT) * jnp.exp(gap), 0.0).astype(BF16)
        mixed_ref[h] = dot(weights, v, NN)
        keyed_hi, keyed_lo = split2(k.astype(F32) * jnp.exp(final - col))
        state = dot(keyed_hi, v, TN) + dot(keyed_lo, v, TN)
        state = state + (first * jnp.exp(final)) * prior_ref[h]
        state_ref[h * HD : (h + 1) * HD, :] = state.astype(BF16)
    state_ref[HEADS_DEV * HD : S_ROWS, :] = decay_lines(finals)
    stores = begin(
        [
            (state_ref, plane_hbm.at[pl.ds(PAY, S_ROWS), :]),
            (mixed_ref, mixed_hbm),
            (cum_ref, cum_hbm),
        ],
        sems,
        11,
    )
    finish(packs)
    finish(stores)


def prep(info, *arrays):
    cum = (TOK, 2 * HEADS_DEV)
    return run(
        prep_kernel,
        "prep",
        (info, *arrays),
        [SMEM] + [HBM] * len(arrays),
        [((PAY, HD), BF16, HBM), ((PAY + S_ROWS, HD), BF16, HBM), (LIN, F32, HBM), (cum, F32, HBM)],
        [
            ((PAY, HD), BF16),
            (LIN, BF16), (LIN, BF16), (LIN, BF16), ((HEADS_DEV, TOK), F32), (STATE, F32),
            (LIN, F32), (cum, F32), ((S_ROWS, HD), BF16),
        ],
        14,
    )


def roll_kernel(info_ref, in_hbm, out_hbm, kv_ref, sems):
    z = info_ref[1] // N_YC
    loads = begin([(in_hbm.at[(z + 1 + i) % N_Z], kv_ref.at[i]) for i in range(N_Z - 1)], sems)
    stores = []
    for i, load in enumerate(loads):
        load.wait()
        stores += begin([(kv_ref.at[i], out_hbm.at[i])], sems, N_Z - 1 + i)
    finish(stores)


def other_planes(info, column):
    shape = (N_Z - 1, PAY, HD)
    return run(
        roll_kernel,
        "other_planes",
        (info, column),
        [SMEM, HBM],
        [(shape, BF16, HBM)],
        [(shape, BF16)],
        2 * (N_Z - 1),
    )


def plane_scan_kernel(info_ref, plane_hbm, own_hbm, own_decay_ref, total_hbm, states, own_ref, total_ref, sems):
    finish(begin([(plane_hbm.at[:, pl.ds(PAY, S_ROWS), :], states)], sems))
    place = info_ref[1] % N_YC
    finals = []
    for h in range(HEADS_DEV):
        rows = slice(h * HD, (h + 1) * HD)
        acc = jnp.zeros((HD, HD), F32)
        run = jnp.zeros((1, HD), F32)
        own, own_run = acc, run
        for r in range(N_YC):
            own = jnp.where(place == r, acc, own)
            own_run = jnp.where(place == r, run, own_run)
            decay = decay_of(states[r, HEADS_DEV * HD : S_ROWS, :], h)
            acc = acc * jnp.exp(decay) + states[r, rows, :].astype(F32)
            run = run + decay
        own_ref[h] = own
        own_decay_ref[h : h + 1, :] = own_run
        total_ref[rows, :] = acc.astype(BF16)
        finals.append(run)
    total_ref[HEADS_DEV * HD : S_ROWS, :] = decay_lines(finals)
    first = (info_ref[1] % N_CORE) * (HEADS_CORE * HD)
    pairs = [(own_ref, own_hbm)]
    for z in range(N_Z):
        pairs.append((total_ref.at[pl.ds(first, HEADS_CORE * HD), :], total_hbm.at[z, pl.ds(0, HEADS_CORE * HD), :]))
        pairs.append(
            (total_ref.at[pl.ds(HEADS_DEV * HD, D_ROWS), :], total_hbm.at[z, pl.ds(HEADS_CORE * HD, D_ROWS), :])
        )
    finish(begin(pairs, sems, 1))


def plane_scan(info, plane):
    return run(
        plane_scan_kernel,
        "plane_scan",
        (info, plane),
        [SMEM, HBM],
        [(STATE, F32, HBM), ((HEADS_DEV, HD), F32, VMEM), ((N_Z, U_ROWS, HD), BF16, HBM)],
        [((N_YC, S_ROWS, HD), BF16), (STATE, F32), ((S_ROWS, HD), BF16)],
        2 + 2 * N_Z,
    )


def lightning_mix_kernel(
    info_ref, q_hbm, mixed_hbm, cum_hbm, own_hbm, own_decay_ref, totals_hbm, prior_hbm,
    out_hbm, square_ref,
    q_ref, mixed_ref, cum_ref, own_ref, totals_ref, prior_ref, out_ref, sems,
):
    loads = begin(
        [
            (totals_hbm, totals_ref), (own_hbm, own_ref), (prior_hbm, prior_ref),
            (cum_hbm, cum_ref), (q_hbm, q_ref), (mixed_hbm, mixed_ref),
        ],
        sems,
    )
    finish(loads)
    place = info_ref[1]
    z_place = place // N_YC
    total = jnp.zeros((TOK, HD), F32)
    for h in range(HEADS_DEV):
        core, inner = h // HEADS_CORE, h % HEADS_CORE
        rows = slice(inner * HD, (inner + 1) * HD)
        acc = jnp.zeros((HD, HD), F32)
        for z in range(N_Z - 1):
            decay = decay_of(totals_ref[core, z, HEADS_CORE * HD : U_ROWS, :], h)
            nxt = acc * jnp.exp(decay) + totals_ref[core, z, rows, :].astype(F32)
            acc = jnp.where(z < z_place, nxt, acc)
        state = own_ref[h] + jnp.exp(own_decay_ref[h : h + 1, :]) * acc
        state = jnp.where(place == 0, prior_ref[h], state)
        hi, low = split2(state)
        q = q_ref[h]
        inter = dot(q, hi, NN) + dot(q, low, NN)
        mixed = mixed_ref[h] + jnp.exp(cum_ref[:, h : h + 1]) * inter
        out_ref[h] = mixed
        total = total + mixed * mixed
    ones = jnp.ones((8, HD), BF16)
    stores = begin([(out_ref, out_hbm)], sems, 6)
    squares = sum(dot(ones, p, NT) for p in split3(total))
    for half in range(TOK // HD):
        line = squares[0:1, half * HD : (half + 1) * HD]
        square_ref[:, half, :] = jnp.broadcast_to(line, (square_ref.shape[0], HD))
    finish(stores)


def lightning_mix(n_tp, info, *arrays):
    specs = [HBM] * len(arrays)
    specs[4] = VMEM
    return run(
        lightning_mix_kernel,
        "lightning_mix",
        (info, *arrays),
        [SMEM] + specs,
        [(LIN, F32, HBM), ((n_tp, TOK // HD, HD), F32, VMEM)],
        [
            (LIN, BF16), (LIN, F32), ((TOK, 2 * HEADS_DEV), F32), (STATE, F32),
            ((N_CORE, N_Z, U_ROWS, HD), BF16), (STATE, F32), (LIN, F32),
        ],
        7,
    )


def norm_kernel(count, mixed_hbm, squares_ref, gain_hbm, out_hbm, mixed_ref, gain_ref, out_ref, sems):
    finish(begin([(mixed_hbm, mixed_ref), (gain_hbm, gain_ref)], sems))
    total = jnp.sum(squares_ref[...], axis=0)
    inv = lax.rsqrt(total * (1.0 / count) + 1e-05)
    t_ids = lax.broadcasted_iota(jnp.int32, (HD, HD), 0)
    s_ids = lax.broadcasted_iota(jnp.int32, (HD, HD), 1)
    for half in range(TOK // HD):
        diag = jnp.where(t_ids == s_ids, jnp.broadcast_to(inv[half : half + 1, :], (HD, HD)), 0.0)
        col = jnp.sum(diag, axis=1, keepdims=True)
        rows = slice(half * HD, (half + 1) * HD)
        for h in range(HEADS_DEV):
            out_ref[h, rows, :] = (mixed_ref[h, rows, :] * col * gain_ref[h : h + 1, :]).astype(BF16)
    finish(begin([(out_ref, out_hbm)], sems, 2))


def lightning_norm(count, mixed, squares, gain):
    return run(
        functools.partial(norm_kernel, float(count)),
        "lightning_norm",
        (mixed, squares, gain),
        [HBM, VMEM, HBM],
        [(LIN, BF16, HBM)],
        [(LIN, F32), ((HEADS_DEV, HD), F32), (LIN, BF16)],
        3,
    )


def cache_bias(info_ref, z, r):
    lanes = lax.broadcasted_iota(jnp.int32, (1, CROWS), 1)
    return jnp.where(lanes < info_ref[2 + z * N_YC + r], 0.0, MASK_FILL).astype(F32)


def with_ones(values):
    return jnp.concatenate([values, jnp.ones(values.shape, BF16)], axis=1)


def wide(stat, width):
    return jnp.concatenate([stat] * (width // HD), axis=1)


def near_kernel(scale, info_ref, q_hbm, plane_hbm, m_hbm, acc_hbm, q_ref, kv, m_ref, acc_ref, sems):
    loads = begin([(q_hbm, q_ref), (plane_hbm.at[:, pl.ds(0, PAY), :], kv)], sems)
    z = info_ref[1] // N_YC
    place = info_ref[1] % N_YC
    rows = lax.broadcasted_iota(jnp.int32, (TOK, TOK), 0)
    cols = lax.broadcasted_iota(jnp.int32, (TOK, TOK), 1)
    ahead = cols - rows
    bias = [cache_bias(info_ref, z, r) for r in range(N_YC)]
    finish(loads)
    stores = []
    keys = kv[:, 0:KROWS, :].reshape(N_YC * KROWS, HD)
    values = with_ones(kv[:, KROWS:PAY, :].reshape(N_YC * KROWS, HD))
    for h in range(HEADS_DEV):
        raw = dot(q_ref[h], keys, NT)
        pieces = []
        for r in range(N_YC):
            span = raw[:, r * KROWS : r * KROWS + TOK]
            pieces.append(jnp.where(ahead <= (place - r) * TOK, span, MASK_FILL))
            pieces.append(raw[:, r * KROWS + TOK : (r + 1) * KROWS] + bias[r])
        raw = jnp.concatenate(pieces, axis=1)
        peak = jnp.broadcast_to(jnp.max(raw, axis=1, keepdims=True), (TOK, HD))
        probs = jnp.exp2((raw - wide(peak, N_YC * KROWS)) * scale)
        m_ref[h] = peak
        acc_ref[h] = dot(probs.astype(BF16), values, NN)
        stores += begin([(m_ref.at[h], m_hbm.at[h]), (acc_ref.at[h], acc_hbm.at[h])], sems, 2 + 2 * h)
    finish(stores)


SUMS = (HEADS_DEV, TOK, 2 * HD)


def near_attention(info, soft_q, plane):
    return run(
        functools.partial(near_kernel, LOG2E / math.sqrt(HD)),
        "near_attention",
        (info, soft_q, plane),
        [SMEM, HBM, HBM],
        [(LIN, F32, HBM), (SUMS, F32, HBM)],
        [(LIN, BF16), ((N_YC, PAY, HD), BF16), (LIN, F32), (SUMS, F32)],
        2 + 2 * HEADS_DEV,
    )


def far_kernel(
    scale, info_ref, q_hbm, m_hbm, acc_hbm, kv_hbm, out_hbm, q_ref, m_ref, acc_ref, kv, out_ref, sems
):
    loads = begin([(q_hbm, q_ref), (m_hbm, m_ref), (acc_hbm, acc_ref)], sems, N_Z - 1)
    begin([(kv_hbm.at[:, i, :, :], kv.at[i]) for i in range(N_Z - 1)], sems)
    finish(loads)
    z_place = info_ref[1] // N_YC

    def update(h, raw, values):
        m_old = m_ref[h]
        m_new = jnp.maximum(m_old, jnp.max(raw, axis=1, keepdims=True))
        probs = jnp.exp2((raw - wide(m_new, raw.shape[1])) * scale)
        alpha = jnp.exp2((m_old - m_new) * scale)
        m_ref[h] = m_new
        acc_ref[h] = acc_ref[h] * wide(alpha, 2 * HD) + dot(probs.astype(BF16), values, NN)

    def fold(i, _):
        pltpu.make_async_copy(kv_hbm.at[:, i, :, :], kv.at[i], sems.at[i]).wait()
        z = (z_place + 1 + i) % N_Z
        bias = [cache_bias(info_ref, z, r) for r in range(N_YC)]

        @pl.when(z < z_place)
        def whole():
            keys = kv[i, :, 0:KROWS, :].reshape(N_YC * KROWS, HD)
            values = with_ones(kv[i, :, KROWS:PAY, :].reshape(N_YC * KROWS, HD))
            for h in range(HEADS_DEV):
                raw = dot(q_ref[h], keys, NT)
                pieces = []
                for r in range(N_YC):
                    pieces.append(raw[:, r * KROWS : r * KROWS + TOK])
                    pieces.append(raw[:, r * KROWS + TOK : (r + 1) * KROWS] + bias[r])
                update(h, jnp.concatenate(pieces, axis=1), values)

        @pl.when(z > z_place)
        def cache_only():
            keys = kv[i, :, TOK:KROWS, :].reshape(N_YC * CROWS, HD)
            values = with_ones(kv[i, :, KROWS + TOK : PAY, :].reshape(N_YC * CROWS, HD))
            line = jnp.concatenate(bias, axis=1)
            for h in range(HEADS_DEV):
                update(h, dot(q_ref[h], keys, NT) + line, values)

        return 0

    lax.fori_loop(0, N_Z - 1, fold, 0)
    stores = []
    for h in range(HEADS_DEV):
        acc = acc_ref[h]
        out_ref[h] = (acc[:, 0:HD] / acc[:, HD : 2 * HD]).astype(BF16)
        stores += begin([(out_ref.at[h], out_hbm.at[h])], sems, N_Z + 2 + h)
    finish(stores)


def far_attention(info, soft_q, peaks, sums, kv):
    return run(
        functools.partial(far_kernel, LOG2E / math.sqrt(HD)),
        "far_attention",
        (info, soft_q, peaks, sums, kv),
        [SMEM] + [HBM] * 4,
        [(LIN, BF16, HBM)],
        [(LIN, BF16), (LIN, F32), (SUMS, F32), ((N_Z - 1, N_YC, PAY, HD), BF16), (LIN, BF16)],
        N_Z + 2 + HEADS_DEV,
    )


def per_device(
    lin_q,
    lin_k,
    lin_v,
    log_decay,
    prior_state,
    lin_gain,
    soft_q,
    span_k,
    span_v,
    cache_k,
    cached_value_rows,
    cache_len,
):
    ctx = lax.axis_index("ctx").astype(jnp.int32)
    tp = lax.axis_index("tp").astype(jnp.int32)
    kv_head = tp * HEADS_DEV // GROUP_Q
    info = jnp.concatenate([kv_head.reshape(1), ctx.reshape(1), cache_len])

    payload, plane_payload, mixed, cum = prep(
        info, span_k, span_v, cache_k, cached_value_rows, lin_q, lin_k, lin_v, log_decay, prior_state
    )
    plane = lax.all_gather(plane_payload, "ctx", axis=0, tiled=True, axis_index_groups=YC_GROUPS)
    plane = plane.reshape(N_YC, PAY + S_ROWS, HD)
    column = lax.all_gather(payload, "ctx", axis=0, tiled=True, axis_index_groups=Z_GROUPS)
    rest = other_planes(info, column.reshape(N_Z, PAY, HD))
    far = lax.all_gather(
        rest.reshape((N_Z - 1) * PAY, HD), "ctx", axis=0, tiled=True, axis_index_groups=YC_GROUPS
    )
    far = far.reshape(N_YC, N_Z - 1, PAY, HD)

    own, own_decay, plane_totals = plane_scan(info, plane)
    totals = lax.all_to_all(plane_totals, "ctx", 0, 0, axis_index_groups=Z_GROUPS)
    totals = lax.all_gather(totals, "ctx", axis=0, axis_index_groups=CORE_GROUPS)
    peaks, sums = near_attention(info, soft_q, plane)
    own, peaks = lax.optimization_barrier((own, peaks))
    n_tp = lax.axis_size("tp")
    mixed, squares = lightning_mix(n_tp, info, lin_q, mixed, cum, own, own_decay, totals, prior_state)
    squares, peaks = lax.optimization_barrier((squares, peaks))
    all_squares = lax.all_to_all(squares, "tp", 0, 0)
    soft_out = far_attention(info, soft_q, peaks, sums, far)
    mixed, soft_out = lax.optimization_barrier((mixed, soft_out))
    normalized = lightning_norm(n_tp * HEADS_DEV * HD, mixed, all_squares, lin_gain)
    return (normalized, soft_out)


def solution(mesh):
    placed = (
        P("tp", "ctx", None),
        P("tp", "ctx", None),
        P("tp", "ctx", None),
        P("tp", "ctx"),
        P("tp", None, None),
        P("tp", None),
        P("tp", "ctx", None),
        P(None, "ctx", None),
        P(None, "ctx", None),
        P(None, "ctx", None),
        P(None, "ctx", None),
        P(),
    )
    return jax.shard_map(
        per_device,
        mesh=mesh,
        in_specs=placed,
        out_specs=(P("tp", "ctx", None), P("tp", "ctx", None)),
        check_vma=False,
    )
```

time: 158 us -> 121 us (0.77)
  the two profiles are of different devices: /device:TPU:408 before, /device:TPU:1 now
where the time goes in v2:
time: 121 us; the launch traced here: 119 us
  blocking collectives  45.4 us (38%)
  Pallas kernels  33.9 us (28%)
  starting transfers between devices  15.2 us (13%)
  between operations  14.2 us (12%)
  waiting for transfers between devices  8.61 us (7%)
  other arithmetic  1.24 us (1%)
    all_gather x1, blocking collectives, per_device(): lax.all_gather(payload, 'ctx', axis=0, tiled=True, axis_index_groups=Z_GR...  38.2 us
    pallas_call x7, Pallas kernels, run(): pl.pallas_call(kernel, out_shape=shapes[0] if single else shapes, in_spec...  33.9 us
    all_to_all x1, starting transfers between devices, per_device(): lax.all_to_all(plane_totals, 'ctx', 0, 0, axis_index_groups=Z_GROUPS)  10.8 us
    all_to_all x1, waiting for transfers between devices, per_device(): lax.all_to_all(plane_totals, 'ctx', 0, 0, axis_index_groups=Z_GROUPS)  8.53 us
    all_gather x1, blocking collectives, per_device(): lax.all_gather(totals, 'ctx', axis=0, axis_index_groups=CORE_GROUPS)  7.17 us
    all_to_all x1, starting transfers between devices, per_device(): all_squares = lax.all_to_all(squares, 'tp', 0, 0)  4.4 us
  transfers between devices with their start and end apart: 4, of which 1 were waited for; matrix products, arithmetic and copies ran while one was open for 0% of the time, Pallas kernels for 23%

profile of v2, /device:TPU:1, one launch (start us, length us, event | category | flops | bytes accessed | tf_op | source)
XLA Modules:
  0.0 119.2 jit_solution(1104421410328900929)
XLA Ops:
  7.2 0.0 all-gather.4.cloned.1.call-start
  7.2 1.2 %pad_add_fusion.info_ref = s32[34]{0:T(128)} fusion(s32[32]{0:T(128)} %param.23, s32[1]{0:T(128)} %bitcast.1, s32[1]{0:T(128)} %bitcast), kind=kLoop, calls=%fused_computation | loop fusion | flops 68 | bytes 272 | tf_op jit(solution)/shard_map/concatenate | solution.py:471
  8.5 4.4 %prep.1 = (bf16[768,128]{1,0:T(8,128)(2,1)}, bf16[1296,128]{1,0:T(8,128)(2,1)}, f32[4,256,128]{2,1,0:T(8,128)}, f32[256,8]{1,0:T(8,128)}) custom-call(s32[34]{0:T(128)} %pad_add_fusion.info_ref, bf16[8,256,128]{2,1,0:T(8,128)(2,1)} %sk_hbm.1, bf16[8,256,128]{2,1,0:T(8,128)(2,1)} %sv_hbm.1, bf16[8,128,128]{2,1,0:T(8,128)(2,1)} %ck_hbm.1, ...), custom_call_target="tpu_custom_call" | custom-call | tf_op jit(solution)/shard_map/prep/pallas_call | solution.py:81
  12.8 0.0 all-gather.4.cloned.1.call-update
  12.9 0.0 all-gather.6.cloned.1.call-start
  12.9 38.2 %all_gather.18 = bf16[3072,128]{1,0:T(8,128)(2,1)} all-gather(bf16[768,128]{1,0:T(8,128)(2,1)} %get-tuple-element.32), channel_id=1, replica_groups={{0,128,256,384},{16,144,272,400},{32,160,288,416},{48,176,304,432},{64,..., dimensions={0}, use_global_device_ids=true | all-gather | bytes 983040 | tf_op jit(solution)/shard_map/all_gather | solution.py:478
  51.1 2.6 %other_planes.1 = bf16[3,768,128]{2,1,0:T(8,128)(2,1)} custom-call(s32[34]{0:T(128)} %pad_add_fusion.info_ref, bf16[4,768,128]{2,1,0:T(8,128)(2,1)} %bitcast.10), custom_call_target="tpu_custom_call" | custom-call | tf_op jit(solution)/shard_map/other_planes/pallas_call | solution.py:81
  53.7 0.0 all-gather.6.cloned.1.call-update
  53.7 0.0 all-gather.4.cloned.1.call-done
  53.8 3.6 %plane_scan.1 = (f32[4,128,128]{2,1,0:T(8,128)}, f32[4,128]{1,0:T(4,128)}, bf16[4,272,128]{2,1,0:T(8,128)(2,1)}) custom-call(s32[34]{0:T(128)} %pad_add_fusion.info_ref, bf16[8,1296,128]{2,1,0:T(8,128)(2,1)} %bitcast.7), custom_call_target="tpu_custom_call" | custom-call | tf_op jit(solution)/shard_map/plane_scan/pallas_call | solution.py:81
  57.3 10.8 %all-to-all-start = ((bf16[4,272,128]{2,1,0:T(8,128)(2,1)}), bf16[4,272,128]{2,1,0:T(8,128)(2,1)S(1)}, u32[]{:S(2)}, u32[]{:S(2)}) async-start(bf16[4,272,128]{2,1,0:T(8,128)(2,1)} %get-tuple-element.26), calls=%async_computation | async-start | bytes 557056 | tf_op jit(solution)/shard_map/all_to_all | solution.py:486
  68.1 8.1 %near_attention.1 = (f32[4,256,128]{2,1,0:T(8,128)}, f32[4,256,256]{2,1,0:T(8,128)}) custom-call(s32[34]{0:T(128)} %pad_add_fusion.info_ref, bf16[4,256,128]{2,1,0:T(8,128)(2,1)} %q_hbm.7, bf16[8,1296,128]{2,1,0:T(8,128)(2,1)} %bitcast.8), custom_call_target="tpu_custom_call" | custom-call | tf_op jit(solution)/shard_map/near_attention/pallas_call | solution.py:81
  76.2 8.5 %all-to-all-done = bf16[4,272,128]{2,1,0:T(8,128)(2,1)S(1)} async-done(((bf16[4,272,128]{2,1,0:T(8,128)(2,1)}), bf16[4,272,128]{2,1,0:T(8,128)(2,1)S(1)}, u32[]{:S(2)}, u32[]{:S(2)}) %all-to-all-start) | async-done | bytes 278560 | tf_op jit(solution)/shard_map/all_to_all | solution.py:486
  84.8 7.2 %all-gather = bf16[8,272,128]{2,1,0:T(8,128)(2,1)} all-gather(bf16[4,272,128]{2,1,0:T(8,128)(2,1)S(1)} %all-to-all-done), channel_id=2, replica_groups={{0,16},{32,48},{64,80},{96,112},{128,144},{160,176},{192,208},{224,240}..., dimensions={0}, use_global_device_ids=true | all-gather | bytes 835584 | tf_op jit(solution)/shard_map/all_gather | solution.py:487
  91.9 4.1 %lightning_mix.1 = (f32[4,256,128]{2,1,0:T(8,128)}, f32[16,2,128]{2,1,0:T(2,128)}) custom-call(s32[34]{0:T(128)} %pad_add_fusion.info_ref, bf16[4,256,128]{2,1,0:T(8,128)(2,1)} %q_hbm.6, f32[4,256,128]{2,1,0:T(8,128)} %get-tuple-element.19.mixed_hbm, f32[256,8]{1,0:T(8,128)} %get-tuple-element.20.cum_hbm, f32[4,128,128]{2,1,0:T(8,128)} %get-tuple-element.24.own_hbm, ...), custom_call_target="tpu_custom_call" | custom-call | tf_op jit(solution)/shard_map/lightning_mix/pallas_call | solution.py:81
  96.0 4.4 %all-to-all-start.1 = ((f32[16,2,128]{2,1,0:T(2,128)}), f32[16,2,128]{2,1,0:T(2,128)S(1)}, u32[]{:S(2)}, u32[]{:S(2)}) async-start(f32[16,2,128]{2,1,0:T(2,128)} %get-tuple-element.34), calls=%async_computation.1 | async-start | bytes 32768 | tf_op jit(solution)/shard_map/all_to_all | solution.py:493
  100.4 0.0 all-gather.6.cloned.1.call-done
  100.4 8.6 %far_attention.1 = bf16[4,256,128]{2,1,0:T(8,128)(2,1)} custom-call(s32[34]{0:T(128)} %pad_add_fusion.info_ref, bf16[4,256,128]{2,1,0:T(8,128)(2,1)} %q_hbm.7, f32[4,256,128]{2,1,0:T(8,128)} %get-tuple-element.30.m_hbm, f32[4,256,256]{2,1,0:T(8,128)} %get-tuple-element.31.acc_hbm, bf16[8,3,768,128]{3,2,1,0:T(8,128)(2,1)} %bitcast.9), custom_call_target="tpu_custom_call" | custom-call | tf_op jit(solution)/shard_map/far_attention/pallas_call | solution.py:81
  109.1 0.0 all-to-all-done.1.squares_ref
  109.1 0.0 copy-start
  109.1 0.6 copy-done
  109.7 2.6 %lightning_norm.1 = bf16[4,256,128]{2,1,0:T(8,128)(2,1)} custom-call(f32[4,256,128]{2,1,0:T(8,128)} %get-tuple-element.33.mixed_hbm, f32[16,2,128]{2,1,0:T(2,128)} %copy-done, f32[4,128]{1,0:T(4,128)} %gain_hbm.1), custom_call_target="tpu_custom_call" | custom-call | tf_op jit(solution)/shard_map/lightning_norm/pallas_call | solution.py:81
Async XLA Ops:
  7.2 46.6 %all-gather.4.cloned.1.call-start = ((), (), s32[]{:S(2)}) async-start(), calls=%async_computation.2 | async-start | bytes 2985984 | tf_op jit(solution)/shard_map/all_gather | solution.py:476
  12.9 87.6 %all-gather.6.cloned.1.call-start = ((), (), s32[]{:S(2)}) async-start(), calls=%async_computation.3 | async-start | bytes 5308416 | tf_op jit(solution)/shard_map/all_gather | solution.py:480
  57.3 27.4 %all-to-all-start = ((bf16[4,272,128]{2,1,0:T(8,128)(2,1)}), bf16[4,272,128]{2,1,0:T(8,128)(2,1)S(1)}, u32[]{:S(2)}, u32[]{:S(2)}) async-start(bf16[4,272,128]{2,1,0:T(8,128)(2,1)} %get-tuple-element.26), calls=%async_computation | async-start | bytes 557056 | tf_op jit(solution)/shard_map/all_to_all | solution.py:486
  96.0 13.1 %all-to-all-start.1 = ((f32[16,2,128]{2,1,0:T(2,128)}), f32[16,2,128]{2,1,0:T(2,128)S(1)}, u32[]{:S(2)}, u32[]{:S(2)}) async-start(f32[16,2,128]{2,1,0:T(2,128)} %get-tuple-element.34), calls=%async_computation.1 | async-start | bytes 32768 | tf_op jit(solution)/shard_map/all_to_all | solution.py:493
  109.1 0.6 copy-start
Sparse Core Ops, SparseCore 0:
  13.0 39.6 all-gather.3
  54.7 43.6 all-gather.5

commit v3 on v2

v3 whole, which is shorter than its diff:
```python
import functools
import math

import jax
import jax.numpy as jnp
from jax import lax
from jax.experimental import pallas as pl
from jax.experimental.pallas import tpu as pltpu
from jax.sharding import PartitionSpec as P

GROUP_Q = 8
N_Z, N_Y, N_CORE = 4, 4, 2
N_CTX = N_Z * N_Y * N_CORE
N_YC = N_Y * N_CORE
N_FAR = N_YC - 1
HD = 128
HEADS_DEV = 4
TOK = 256
CROWS = 128
KROWS = TOK + CROWS
PAY = 2 * KROWS
D_ROWS = 16
S_ROWS = HEADS_DEV * HD + D_ROWS
HEADS_CORE = HEADS_DEV // N_CORE
U_ROWS = HEADS_CORE * HD + D_ROWS
MASK_FILL = -1e30
LOG2E = 1.4426950408889634
VMEM_LIMIT = 60 * 1024 * 1024

F32 = jnp.float32
BF16 = jnp.bfloat16

Z_GROUPS = [[z * N_YC + r for z in range(N_Z)] for r in range(N_YC)]
YC_GROUPS = [[z * N_YC + r for r in range(N_YC)] for z in range(N_Z)]
CORE_GROUPS = [[N_CORE * r + i for i in range(N_CORE)] for r in range(N_CTX // N_CORE)]

NT = (((1,), (1,)), ((), ()))
NN = (((1,), (0,)), ((), ()))
TN = (((0,), (0,)), ((), ()))


def dot(a, b, dims):
    return lax.dot_general(a, b, dims, preferred_element_type=F32)


def split3(x):
    hi = x.astype(BF16)
    rest = x - hi.astype(F32)
    mid = rest.astype(BF16)
    low = (rest - mid.astype(F32)).astype(BF16)
    return hi, mid, low


def split2(x):
    hi = x.astype(BF16)
    return hi, (x - hi.astype(F32)).astype(BF16)


HBM = pl.BlockSpec(memory_space=pltpu.HBM)
VMEM = pl.BlockSpec(memory_space=pltpu.VMEM)
SMEM = pl.BlockSpec(memory_space=pltpu.SMEM)
LIN = (HEADS_DEV, TOK, HD)
STATE = (HEADS_DEV, HD, HD)
CUM = (TOK, 2 * HEADS_DEV)


def ctx_place():
    return lax.axis_index("ctx").astype(jnp.int32)


def begin(pairs, sems, base=0):
    copies = [pltpu.make_async_copy(a, b, sems.at[base + i]) for i, (a, b) in enumerate(pairs)]
    for copy in copies:
        copy.start()
    return copies


def finish(copies):
    for copy in copies:
        copy.wait()


def run(kernel, name, operands, in_specs, outs, scratch, n_sems):
    single = len(outs) == 1
    shapes = tuple(jax.ShapeDtypeStruct(shape, kind) for shape, kind, _ in outs)
    specs = tuple(spec for _, _, spec in outs)
    return pl.pallas_call(
        kernel,
        out_shape=shapes[0] if single else shapes,
        in_specs=in_specs,
        out_specs=specs[0] if single else specs,
        scratch_shapes=[pltpu.VMEM(shape, kind) for shape, kind in scratch]
        + [pltpu.SemaphoreType.DMA((n_sems,))],
        compiler_params=pltpu.CompilerParams(vmem_limit_bytes=VMEM_LIMIT),
        name=name,
    )(*operands)


def decay_lines(values):
    ids = lax.broadcasted_iota(jnp.int32, (D_ROWS, HD), 0)
    lines = jnp.zeros((D_ROWS, HD), F32)
    for h, value in enumerate(values):
        for i, part in enumerate(split3(jnp.broadcast_to(value, (1, HD)))):
            lines = jnp.where(ids == 3 * h + i, part.astype(F32), lines)
    return lines.astype(BF16)


def decay_of(lines, h):
    lines = lines[3 * h : 3 * h + 3].astype(F32)
    return lines[0:1] + lines[1:2] + lines[2:3]


def decay_sums(decay_ref):
    t_ids = lax.broadcasted_iota(jnp.int32, (TOK, TOK), 0)
    s_ids = lax.broadcasted_iota(jnp.int32, (TOK, TOK), 1)
    lower = t_ids >= s_ids
    tri = jnp.where(lower, 1.0, 0.0).astype(BF16)
    parts = split3(jnp.concatenate([decay_ref[...], decay_ref[...]], axis=0))
    cum_rows = sum(dot(p, tri, NT) for p in parts)
    cum_cols = sum(dot(tri, p, NT) for p in parts)
    return lower, cum_rows, cum_cols


def prep_kernel(
    sk_hbm, sv_hbm, ck_hbm, cv_hbm, k_hbm, v_hbm, decay_hbm, prior_hbm,
    payload_hbm, plane_hbm,
    kv_ref, k_ref, v_ref, decay_ref, prior_ref, state_ref, sems,
):
    head = lax.axis_index("tp").astype(jnp.int32) * HEADS_DEV // GROUP_Q
    loads = begin(
        [(decay_hbm, decay_ref), (k_hbm, k_ref), (v_hbm, v_ref), (prior_hbm, prior_ref)], sems
    )
    packs = begin(
        [
            (sk_hbm.at[head], kv_ref.at[pl.ds(0, TOK), :]),
            (ck_hbm.at[head], kv_ref.at[pl.ds(TOK, CROWS), :]),
            (sv_hbm.at[head], kv_ref.at[pl.ds(KROWS, TOK), :]),
            (cv_hbm.at[head], kv_ref.at[pl.ds(KROWS + TOK, CROWS), :]),
        ],
        sems,
        4,
    )
    first = jnp.where(ctx_place() == 0, 1.0, 0.0).astype(F32)
    loads[0].wait()
    _, cum_rows, cum_cols = decay_sums(decay_ref)
    finish(packs)
    packs = begin([(kv_ref, payload_hbm), (kv_ref, plane_hbm.at[pl.ds(0, PAY), :])], sems, 8)
    finish(loads[1:])
    finals = []
    for h in range(HEADS_DEV):
        col = cum_cols[:, h : h + 1]
        final = cum_rows[h : h + 1, TOK - 1 : TOK]
        finals.append(final)
        v = v_ref[h]
        keyed_hi, keyed_lo = split2(k_ref[h].astype(F32) * jnp.exp(final - col))
        state = dot(keyed_hi, v, TN) + dot(keyed_lo, v, TN)
        state = state + (first * jnp.exp(final)) * prior_ref[h]
        state_ref[h * HD : (h + 1) * HD, :] = state.astype(BF16)
    state_ref[HEADS_DEV * HD : S_ROWS, :] = decay_lines(finals)
    stores = begin([(state_ref, plane_hbm.at[pl.ds(PAY, S_ROWS), :])], sems, 10)
    finish(packs)
    finish(stores)


def prep(*arrays):
    return run(
        prep_kernel,
        "prep",
        arrays,
        [HBM] * len(arrays),
        [((PAY, HD), BF16, HBM), ((PAY + S_ROWS, HD), BF16, HBM)],
        [
            ((PAY, HD), BF16), (LIN, BF16), (LIN, BF16), ((HEADS_DEV, TOK), F32), (STATE, F32),
            ((S_ROWS, HD), BF16),
        ],
        11,
    )


def roll_kernel(in_hbm, out_hbm, kv_ref, sems):
    z = ctx_place() // N_YC
    loads = begin([(in_hbm.at[(z + 1 + i) % N_Z], kv_ref.at[i]) for i in range(N_Z - 1)], sems)
    stores = []
    for i, load in enumerate(loads):
        load.wait()
        stores += begin([(kv_ref.at[i], out_hbm.at[i])], sems, N_Z - 1 + i)
    finish(stores)


def other_planes(column):
    shape = (N_Z - 1, PAY, HD)
    return run(
        roll_kernel,
        "other_planes",
        (column,),
        [HBM],
        [(shape, BF16, HBM)],
        [(shape, BF16)],
        2 * (N_Z - 1),
    )


def plane_scan_kernel(plane_hbm, own_hbm, own_decay_ref, total_hbm, states, own_ref, total_ref, sems):
    finish(begin([(plane_hbm.at[:, pl.ds(PAY, S_ROWS), :], states)], sems))
    place = ctx_place() % N_YC
    finals = []
    for h in range(HEADS_DEV):
        rows = slice(h * HD, (h + 1) * HD)
        acc = jnp.zeros((HD, HD), F32)
        run = jnp.zeros((1, HD), F32)
        own, own_run = acc, run
        for r in range(N_YC):
            own = jnp.where(place == r, acc, own)
            own_run = jnp.where(place == r, run, own_run)
            decay = decay_of(states[r, HEADS_DEV * HD : S_ROWS, :], h)
            acc = acc * jnp.exp(decay) + states[r, rows, :].astype(F32)
            run = run + decay
        own_ref[h] = own
        own_decay_ref[h : h + 1, :] = own_run
        total_ref[rows, :] = acc.astype(BF16)
        finals.append(run)
    total_ref[HEADS_DEV * HD : S_ROWS, :] = decay_lines(finals)
    first = (ctx_place() % N_CORE) * (HEADS_CORE * HD)
    pairs = [(own_ref, own_hbm)]
    for z in range(N_Z):
        pairs.append((total_ref.at[pl.ds(first, HEADS_CORE * HD), :], total_hbm.at[z, pl.ds(0, HEADS_CORE * HD), :]))
        pairs.append(
            (total_ref.at[pl.ds(HEADS_DEV * HD, D_ROWS), :], total_hbm.at[z, pl.ds(HEADS_CORE * HD, D_ROWS), :])
        )
    finish(begin(pairs, sems, 1))


def plane_scan(plane):
    return run(
        plane_scan_kernel,
        "plane_scan",
        (plane,),
        [HBM],
        [(STATE, F32, HBM), ((HEADS_DEV, HD), F32, VMEM), ((N_Z, U_ROWS, HD), BF16, HBM)],
        [((N_YC, S_ROWS, HD), BF16), (STATE, F32), ((S_ROWS, HD), BF16)],
        2 + 2 * N_Z,
    )


def lightning_mix_kernel(
    q_hbm, mixed_hbm, cum_hbm, own_hbm, own_decay_ref, totals_hbm, prior_hbm,
    out_hbm, square_ref,
    q_ref, mixed_ref, cum_ref, own_ref, totals_ref, prior_ref, out_ref, sems,
):
    loads = begin(
        [
            (totals_hbm, totals_ref), (own_hbm, own_ref), (prior_hbm, prior_ref),
            (cum_hbm, cum_ref), (q_hbm, q_ref), (mixed_hbm, mixed_ref),
        ],
        sems,
    )
    place = ctx_place()
    z_place = place // N_YC
    finish(loads)
    stores = []
    total = jnp.zeros((TOK, HD), F32)
    for h in range(HEADS_DEV):
        core, inner = h // HEADS_CORE, h % HEADS_CORE
        rows = slice(inner * HD, (inner + 1) * HD)
        acc = jnp.zeros((HD, HD), F32)
        for z in range(N_Z - 1):
            decay = decay_of(totals_ref[core, z, HEADS_CORE * HD : U_ROWS, :], h)
            nxt = acc * jnp.exp(decay) + totals_ref[core, z, rows, :].astype(F32)
            acc = jnp.where(z < z_place, nxt, acc)
        state = own_ref[h] + jnp.exp(own_decay_ref[h : h + 1, :]) * acc
        state = jnp.where(place == 0, prior_ref[h], state)
        hi, low = split2(state)
        q = q_ref[h]
        inter = dot(q, hi, NN) + dot(q, low, NN)
        mixed = mixed_ref[h] + jnp.exp(cum_ref[:, h : h + 1]) * inter
        out_ref[h] = mixed
        stores += begin([(out_ref.at[h], out_hbm.at[h])], sems, 6 + h)
        total = total + mixed * mixed
    ones = jnp.ones((8, HD), BF16)
    squares = sum(dot(ones, p, NT) for p in split3(total))
    for half in range(TOK // HD):
        line = squares[0:1, half * HD : (half + 1) * HD]
        square_ref[:, half, :] = jnp.broadcast_to(line, (square_ref.shape[0], HD))
    finish(stores)


def lightning_mix(n_tp, *arrays):
    specs = [HBM] * len(arrays)
    specs[4] = VMEM
    return run(
        lightning_mix_kernel,
        "lightning_mix",
        arrays,
        specs,
        [(LIN, F32, HBM), ((n_tp, TOK // HD, HD), F32, VMEM)],
        [
            (LIN, BF16), (LIN, F32), (CUM, F32), (STATE, F32),
            ((N_CORE, N_Z, U_ROWS, HD), BF16), (STATE, F32), (LIN, F32),
        ],
        6 + HEADS_DEV,
    )


def norm_kernel(count, mixed_hbm, squares_ref, gain_hbm, out_hbm, mixed_ref, gain_ref, out_ref, sems):
    finish(begin([(mixed_hbm, mixed_ref), (gain_hbm, gain_ref)], sems))
    total = jnp.sum(squares_ref[...], axis=0)
    inv = lax.rsqrt(total * (1.0 / count) + 1e-05)
    t_ids = lax.broadcasted_iota(jnp.int32, (HD, HD), 0)
    s_ids = lax.broadcasted_iota(jnp.int32, (HD, HD), 1)
    for half in range(TOK // HD):
        diag = jnp.where(t_ids == s_ids, jnp.broadcast_to(inv[half : half + 1, :], (HD, HD)), 0.0)
        col = jnp.sum(diag, axis=1, keepdims=True)
        rows = slice(half * HD, (half + 1) * HD)
        for h in range(HEADS_DEV):
            out_ref[h, rows, :] = (mixed_ref[h, rows, :] * col * gain_ref[h : h + 1, :]).astype(BF16)
    finish(begin([(out_ref, out_hbm)], sems, 2))


def lightning_norm(count, mixed, squares, gain):
    return run(
        functools.partial(norm_kernel, float(count)),
        "lightning_norm",
        (mixed, squares, gain),
        [HBM, VMEM, HBM],
        [(LIN, BF16, HBM)],
        [(LIN, F32), ((HEADS_DEV, HD), F32), (LIN, BF16)],
        3,
    )


def cache_bias(len_ref, z, r):
    lanes = lax.broadcasted_iota(jnp.int32, (1, CROWS), 1)
    return jnp.where(lanes < len_ref[z * N_YC + r], 0.0, MASK_FILL).astype(F32)


def with_ones(values):
    return jnp.concatenate([values, jnp.ones(values.shape, BF16)], axis=1)


def wide(stat, width):
    return jnp.concatenate([stat] * (width // HD), axis=1)


def near_kernel(
    scale,
    len_ref, q_hbm, plane_hbm, rest_hbm, lq_hbm, lk_hbm, lv_hbm, decay_hbm,
    m_hbm, acc_hbm, mixed_hbm, cum_hbm,
    q_ref, kv, kr, lq_ref, lk_ref, lv_ref, decay_ref, m_ref, acc_ref, mixed_ref, cum_ref, sems,
):
    loads = begin(
        [
            (decay_hbm, decay_ref), (lq_hbm, lq_ref), (lk_hbm, lk_ref), (lv_hbm, lv_ref),
            (q_hbm, q_ref), (plane_hbm.at[:, pl.ds(0, PAY), :], kv), (rest_hbm, kr),
        ],
        sems,
    )
    n_loads = len(loads)
    z = ctx_place() // N_YC
    place = ctx_place() % N_YC
    finish(loads[:4])
    lower, cum_rows, cum_cols = decay_sums(decay_ref)
    cum_ref[...] = cum_cols
    for h in range(HEADS_DEV):
        gap = jnp.where(lower, cum_cols[:, h : h + 1] - cum_rows[h : h + 1, :], 0.0)
        weights = jnp.where(lower, dot(lq_ref[h], lk_ref[h], NT) * jnp.exp(gap), 0.0).astype(BF16)
        mixed_ref[h] = dot(weights, lv_ref[h], NN)
    stores = begin([(mixed_ref, mixed_hbm), (cum_ref, cum_hbm)], sems, n_loads)

    rows = lax.broadcasted_iota(jnp.int32, (TOK, TOK), 0)
    cols = lax.broadcasted_iota(jnp.int32, (TOK, TOK), 1)
    ahead = cols - rows
    bias = [cache_bias(len_ref, z, r) for r in range(N_YC)]
    line = []
    for i in range(N_Z - 1):
        other = (z + 1 + i) % N_Z
        line.append(jnp.full((1, TOK), jnp.where(other < z, 0.0, MASK_FILL).astype(F32)))
        line.append(cache_bias(len_ref, other, place))
    line = jnp.concatenate(line, axis=1)
    finish(loads[4:])
    keys = kv[:, 0:KROWS, :].reshape(N_YC * KROWS, HD)
    values = with_ones(kv[:, KROWS:PAY, :].reshape(N_YC * KROWS, HD))
    column_keys = kr[:, 0:KROWS, :].reshape((N_Z - 1) * KROWS, HD)
    column_values = with_ones(kr[:, KROWS:PAY, :].reshape((N_Z - 1) * KROWS, HD))
    for h in range(HEADS_DEV):
        raw = dot(q_ref[h], keys, NT)
        pieces = []
        for r in range(N_YC):
            span = raw[:, r * KROWS : r * KROWS + TOK]
            pieces.append(jnp.where(ahead <= (place - r) * TOK, span, MASK_FILL))
            pieces.append(raw[:, r * KROWS + TOK : (r + 1) * KROWS] + bias[r])
        raw = jnp.concatenate(pieces, axis=1)
        column_raw = dot(q_ref[h], column_keys, NT) + line
        peak = jnp.maximum(
            jnp.max(raw, axis=1, keepdims=True), jnp.max(column_raw, axis=1, keepdims=True)
        )
        peak = jnp.broadcast_to(peak, (TOK, HD))
        probs = jnp.exp2((raw - wide(peak, raw.shape[1])) * scale).astype(BF16)
        column_probs = jnp.exp2((column_raw - wide(peak, column_raw.shape[1])) * scale).astype(BF16)
        m_ref[h] = peak
        acc_ref[h] = dot(probs, values, NN) + dot(column_probs, column_values, NN)
        stores += begin(
            [(m_ref.at[h], m_hbm.at[h]), (acc_ref.at[h], acc_hbm.at[h])], sems, n_loads + 2 + 2 * h
        )
    finish(stores)


SUMS = (HEADS_DEV, TOK, 2 * HD)


def near_work(cache_len, *arrays):
    return run(
        functools.partial(near_kernel, LOG2E / math.sqrt(HD)),
        "near_work",
        (cache_len, *arrays),
        [SMEM] + [HBM] * len(arrays),
        [(LIN, F32, HBM), (SUMS, F32, HBM), (LIN, F32, HBM), (CUM, F32, HBM)],
        [
            (LIN, BF16), ((N_YC, PAY, HD), BF16), ((N_Z - 1, PAY, HD), BF16),
            (LIN, BF16), (LIN, BF16), (LIN, BF16), ((HEADS_DEV, TOK), F32),
            (LIN, F32), (SUMS, F32), (LIN, F32), (CUM, F32),
        ],
        9 + 2 * HEADS_DEV,
    )


def far_kernel(
    scale, len_ref, q_hbm, m_hbm, acc_hbm, kv_hbm, out_hbm, q_ref, m_ref, acc_ref, kv, out_ref, sems
):
    z_place = ctx_place() // N_YC
    place = ctx_place() % N_YC
    others = [(place + 1 + j) % N_YC for j in range(N_FAR)]
    loads = begin([(q_hbm, q_ref), (m_hbm, m_ref), (acc_hbm, acc_ref)], sems)
    blocks = []
    for i in range(N_Z - 1):
        pairs = [(kv_hbm.at[r, i], kv.at[i, j]) for j, r in enumerate(others)]
        blocks.append(begin(pairs, sems, 3 + i * N_FAR))
    finish(loads)

    def update(h, raw, values):
        m_old = m_ref[h]
        m_new = jnp.maximum(m_old, jnp.max(raw, axis=1, keepdims=True))
        probs = jnp.exp2((raw - wide(m_new, raw.shape[1])) * scale)
        alpha = jnp.exp2((m_old - m_new) * scale)
        m_ref[h] = m_new
        acc_ref[h] = acc_ref[h] * wide(alpha, 2 * HD) + dot(probs.astype(BF16), values, NN)

    for i in range(N_Z - 1):
        finish(blocks[i])
        z = (z_place + 1 + i) % N_Z
        bias = [cache_bias(len_ref, z, r) for r in others]

        @pl.when(z < z_place)
        def whole():
            keys = kv[i, :, 0:KROWS, :].reshape(N_FAR * KROWS, HD)
            values = with_ones(kv[i, :, KROWS:PAY, :].reshape(N_FAR * KROWS, HD))
            for h in range(HEADS_DEV):
                raw = dot(q_ref[h], keys, NT)
                pieces = []
                for r in range(N_FAR):
                    pieces.append(raw[:, r * KROWS : r * KROWS + TOK])
                    pieces.append(raw[:, r * KROWS + TOK : (r + 1) * KROWS] + bias[r])
                update(h, jnp.concatenate(pieces, axis=1), values)

        @pl.when(z > z_place)
        def cache_only():
            keys = kv[i, :, TOK:KROWS, :].reshape(N_FAR * CROWS, HD)
            values = with_ones(kv[i, :, KROWS + TOK : PAY, :].reshape(N_FAR * CROWS, HD))
            line = jnp.concatenate(bias, axis=1)
            for h in range(HEADS_DEV):
                update(h, dot(q_ref[h], keys, NT) + line, values)

    stores = []
    for h in range(HEADS_DEV):
        acc = acc_ref[h]
        out_ref[h] = (acc[:, 0:HD] / acc[:, HD : 2 * HD]).astype(BF16)
        stores += begin([(out_ref.at[h], out_hbm.at[h])], sems, 3 + (N_Z - 1) * N_FAR + h)
    finish(stores)


def far_attention(cache_len, soft_q, peaks, sums, kv):
    return run(
        functools.partial(far_kernel, LOG2E / math.sqrt(HD)),
        "far_attention",
        (cache_len, soft_q, peaks, sums, kv),
        [SMEM] + [HBM] * 4,
        [(LIN, BF16, HBM)],
        [(LIN, BF16), (LIN, F32), (SUMS, F32), ((N_Z - 1, N_FAR, PAY, HD), BF16), (LIN, BF16)],
        3 + (N_Z - 1) * N_FAR + HEADS_DEV,
    )


def per_device(
    lin_q,
    lin_k,
    lin_v,
    log_decay,
    prior_state,
    lin_gain,
    soft_q,
    span_k,
    span_v,
    cache_k,
    cached_value_rows,
    cache_len,
):
    payload, plane_payload = prep(
        span_k, span_v, cache_k, cached_value_rows, lin_k, lin_v, log_decay, prior_state
    )
    plane = lax.all_gather(plane_payload, "ctx", axis=0, tiled=True, axis_index_groups=YC_GROUPS)
    plane = plane.reshape(N_YC, PAY + S_ROWS, HD)
    column = lax.all_gather(payload, "ctx", axis=0, tiled=True, axis_index_groups=Z_GROUPS)
    rest = other_planes(column.reshape(N_Z, PAY, HD))
    far = lax.all_gather(
        rest.reshape((N_Z - 1) * PAY, HD), "ctx", axis=0, tiled=True, axis_index_groups=YC_GROUPS
    )
    far = far.reshape(N_YC, N_Z - 1, PAY, HD)

    own, own_decay, plane_totals = plane_scan(plane)
    totals = lax.all_to_all(plane_totals, "ctx", 0, 0, axis_index_groups=Z_GROUPS)
    totals = lax.all_gather(totals, "ctx", axis=0, axis_index_groups=CORE_GROUPS)
    peaks, sums, mixed, cum = near_work(
        cache_len, soft_q, plane, rest, lin_q, lin_k, lin_v, log_decay
    )
    own, peaks = lax.optimization_barrier((own, peaks))
    n_tp = lax.axis_size("tp")
    mixed, squares = lightning_mix(
        n_tp, lin_q, mixed, cum, own, own_decay, totals, prior_state
    )
    squares, peaks = lax.optimization_barrier((squares, peaks))
    all_squares = lax.all_to_all(squares, "tp", 0, 0)
    soft_out = far_attention(cache_len, soft_q, peaks, sums, far)
    mixed, soft_out = lax.optimization_barrier((mixed, soft_out))
    normalized = lightning_norm(n_tp * HEADS_DEV * HD, mixed, all_squares, lin_gain)
    return (normalized, soft_out)


def solution(mesh):
    placed = (
        P("tp", "ctx", None),
        P("tp", "ctx", None),
        P("tp", "ctx", None),
        P("tp", "ctx"),
        P("tp", None, None),
        P("tp", None),
        P("tp", "ctx", None),
        P(None, "ctx", None),
        P(None, "ctx", None),
        P(None, "ctx", None),
        P(None, "ctx", None),
        P(),
    )
    return jax.shard_map(
        per_device,
        mesh=mesh,
        in_specs=placed,
        out_specs=(P("tp", "ctx", None), P("tp", "ctx", None)),
        check_vma=False,
    )
```

time: 121 us -> 117 us (0.967)
  waiting for transfers between devices: 8.61 us -> 4.95 us
  other arithmetic: 1.24 us -> 0 us
    all_to_all x1, waiting for transfers between devices: 8.53 us -> 4.87 us  [per_device(): lax.all_to_all(plane_totals, 'ctx', 0, 0, axis_index_groups=Z_GROUPS)]
    concatenate x1 -> x0, other arithmetic: 1.24 us -> none  [per_device(): info = jnp.concatenate([kv_head.reshape(1), ctx.reshape(1), cache_len])]
  transfers between devices with their start and end apart: 4 -> 4, of which waited for: 1 -> 1; matrix products, arithmetic and copies ran while one was open for 0% -> 0% of each run, Pallas kernels for 23% -> 25%
where the time goes in v3:
time: 117 us; the launch traced here: 116 us
  blocking collectives  46.5 us (40%)
  Pallas kernels  34.4 us (29%)
  starting transfers between devices  15.4 us (13%)
  between operations  14.1 us (12%)
  waiting for transfers between devices  4.95 us (4%)
    all_gather x1, blocking collectives, per_device(): lax.all_gather(payload, 'ctx', axis=0, tiled=True, axis_index_groups=Z_GR...  39.1 us
    pallas_call x7, Pallas kernels, run(): pl.pallas_call(kernel, out_shape=shapes[0] if single else shapes, in_spec...  34.4 us
    all_to_all x1, starting transfers between devices, per_device(): lax.all_to_all(plane_totals, 'ctx', 0, 0, axis_index_groups=Z_GROUPS)  10.6 us
    all_gather x1, blocking collectives, per_device(): lax.all_gather(totals, 'ctx', axis=0, axis_index_groups=CORE_GROUPS)  7.4 us
    all_to_all x1, waiting for transfers between devices, per_device(): lax.all_to_all(plane_totals, 'ctx', 0, 0, axis_index_groups=Z_GROUPS)  4.87 us
    all_to_all x1, starting transfers between devices, per_device(): all_squares = lax.all_to_all(squares, 'tp', 0, 0)  4.67 us
  transfers between devices with their start and end apart: 4, of which 1 were waited for; matrix products, arithmetic and copies ran while one was open for 0% of the time, Pallas kernels for 25%

profile of v3, /device:TPU:1, one launch (start us, length us, event | category | flops | bytes accessed | tf_op | source)
XLA Modules:
  0.0 116.0 jit_solution(15342945069446224161)
XLA Ops:
  7.2 0.0 all-gather.4.cloned.1.call-start
  7.2 2.7 %prep.1 = (bf16[768,128]{1,0:T(8,128)(2,1)}, bf16[1296,128]{1,0:T(8,128)(2,1)}) custom-call(bf16[8,256,128]{2,1,0:T(8,128)(2,1)} %sk_hbm.1, bf16[8,256,128]{2,1,0:T(8,128)(2,1)} %sv_hbm.1, bf16[8,128,128]{2,1,0:T(8,128)(2,1)} %ck_hbm.1, bf16[8,128,128]{2,1,0:T(8,128)(2,1)} %cv_hbm.1, bf16[4,256,128]{2,1,0:T(8,128)(2,1)} %lk_hbm.1, ...), custom_call_target="tpu_custom_call" | custom-call | tf_op jit(solution)/shard_map/prep/pallas_call | solution.py:87
  9.9 0.0 all-gather.4.cloned.1.call-update
  9.9 0.0 all-gather.6.cloned.1.call-start
  10.0 39.1 %all_gather.16 = bf16[3072,128]{1,0:T(8,128)(2,1)} all-gather(bf16[768,128]{1,0:T(8,128)(2,1)} %get-tuple-element.20), channel_id=1, replica_groups={{0,128,256,384},{16,144,272,400},{32,160,288,416},{48,176,304,432},{64,..., dimensions={0}, use_global_device_ids=true | all-gather | bytes 983040 | tf_op jit(solution)/shard_map/all_gather | solution.py:511
  49.1 1.9 %other_planes.1.rest_hbm = bf16[3,768,128]{2,1,0:T(8,128)(2,1)} custom-call(bf16[4,768,128]{2,1,0:T(8,128)(2,1)} %bitcast.9), custom_call_target="tpu_custom_call" | custom-call | tf_op jit(solution)/shard_map/other_planes/pallas_call | solution.py:87
  51.0 0.0 all-gather.6.cloned.1.call-update
  51.0 0.0 all-gather.4.cloned.1.call-done
  51.1 2.9 %plane_scan.1 = (f32[4,128,128]{2,1,0:T(8,128)}, f32[4,128]{1,0:T(4,128)}, bf16[4,272,128]{2,1,0:T(8,128)(2,1)}) custom-call(bf16[8,1296,128]{2,1,0:T(8,128)(2,1)} %bitcast.5), custom_call_target="tpu_custom_call" | custom-call | tf_op jit(solution)/shard_map/plane_scan/pallas_call | solution.py:87
  54.0 10.6 %all-to-all-start = ((bf16[4,272,128]{2,1,0:T(8,128)(2,1)}), bf16[4,272,128]{2,1,0:T(8,128)(2,1)S(1)}, u32[]{:S(2)}, u32[]{:S(2)}) async-start(bf16[4,272,128]{2,1,0:T(8,128)(2,1)} %get-tuple-element.27), calls=%async_computation | async-start | bytes 557056 | tf_op jit(solution)/shard_map/all_to_all | solution.py:519
  64.6 11.4 %near_work.1 = (f32[4,256,128]{2,1,0:T(8,128)}, f32[4,256,256]{2,1,0:T(8,128)}, f32[4,256,128]{2,1,0:T(8,128)}, f32[256,8]{1,0:T(8,128)}) custom-call(s32[32]{0:T(128)} %len_ref.3, bf16[4,256,128]{2,1,0:T(8,128)(2,1)} %q_hbm.5, bf16[8,1296,128]{2,1,0:T(8,128)(2,1)} %bitcast.6, bf16[3,768,128]{2,1,0:T(8,128)(2,1)} %other_planes.1.rest_hbm, ...), custom_call_target="tpu_custom_call" | custom-call | tf_op jit(solution)/shard_map/near_work/pallas_call | solution.py:87
  76.0 4.9 %all-to-all-done = bf16[4,272,128]{2,1,0:T(8,128)(2,1)S(1)} async-done(((bf16[4,272,128]{2,1,0:T(8,128)(2,1)}), bf16[4,272,128]{2,1,0:T(8,128)(2,1)S(1)}, u32[]{:S(2)}, u32[]{:S(2)}) %all-to-all-start) | async-done | bytes 278560 | tf_op jit(solution)/shard_map/all_to_all | solution.py:519
  80.9 7.4 %all-gather = bf16[8,272,128]{2,1,0:T(8,128)(2,1)} all-gather(bf16[4,272,128]{2,1,0:T(8,128)(2,1)S(1)} %all-to-all-done), channel_id=2, replica_groups={{0,16},{32,48},{64,80},{96,112},{128,144},{160,176},{192,208},{224,240}..., dimensions={0}, use_global_device_ids=true | all-gather | bytes 835584 | tf_op jit(solution)/shard_map/all_gather | solution.py:520
  88.3 4.0 %lightning_mix.1 = (f32[4,256,128]{2,1,0:T(8,128)}, f32[16,2,128]{2,1,0:T(2,128)}) custom-call(bf16[4,256,128]{2,1,0:T(8,128)(2,1)} %q_hbm.4, f32[4,256,128]{2,1,0:T(8,128)} %get-tuple-element.21.mixed_hbm, f32[256,8]{1,0:T(8,128)} %get-tuple-element.22.cum_hbm, f32[4,128,128]{2,1,0:T(8,128)} %get-tuple-element.25.own_hbm, ...), custom_call_target="tpu_custom_call" | custom-call | tf_op jit(solution)/shard_map/lightning_mix/pallas_call | solution.py:87
  92.3 4.7 %all-to-all-start.1 = ((f32[16,2,128]{2,1,0:T(2,128)}), f32[16,2,128]{2,1,0:T(2,128)S(1)}, u32[]{:S(2)}, u32[]{:S(2)}) async-start(f32[16,2,128]{2,1,0:T(2,128)} %get-tuple-element.34), calls=%async_computation.1 | async-start | bytes 32768 | tf_op jit(solution)/shard_map/all_to_all | solution.py:530
  97.0 0.0 all-gather.6.cloned.1.call-done
  97.0 8.9 %far_attention.1 = bf16[4,256,128]{2,1,0:T(8,128)(2,1)} custom-call(s32[32]{0:T(128)} %len_ref.3, bf16[4,256,128]{2,1,0:T(8,128)(2,1)} %q_hbm.5, f32[4,256,128]{2,1,0:T(8,128)} %get-tuple-element.31.m_hbm, f32[4,256,256]{2,1,0:T(8,128)} %get-tuple-element.32.acc_hbm, bf16[8,3,768,128]{3,2,1,0:T(8,128)(2,1)} %bitcast.8), custom_call_target="tpu_custom_call" | custom-call | tf_op jit(solution)/shard_map/far_attention/pallas_call | solution.py:87
  105.9 0.0 all-to-all-done.1.squares_ref
  105.9 0.0 copy-start
  105.9 0.6 copy-done
  106.5 2.6 %lightning_norm.1 = bf16[4,256,128]{2,1,0:T(8,128)(2,1)} custom-call(f32[4,256,128]{2,1,0:T(8,128)} %get-tuple-element.33.mixed_hbm, f32[16,2,128]{2,1,0:T(2,128)} %copy-done, f32[4,128]{1,0:T(4,128)} %gain_hbm.1), custom_call_target="tpu_custom_call" | custom-call | tf_op jit(solution)/shard_map/lightning_norm/pallas_call | solution.py:87
Async XLA Ops:
  7.2 43.9 %all-gather.4.cloned.1.call-start = ((), (), s32[]{:S(2)}) async-start(), calls=%async_computation.2 | async-start | bytes 2985984 | tf_op jit(solution)/shard_map/all_gather | solution.py:509
  9.9 87.0 %all-gather.6.cloned.1.call-start = ((), (), s32[]{:S(2)}) async-start(), calls=%async_computation.3 | async-start | bytes 5308416 | tf_op jit(solution)/shard_map/all_gather | solution.py:513
  54.0 26.9 %all-to-all-start = ((bf16[4,272,128]{2,1,0:T(8,128)(2,1)}), bf16[4,272,128]{2,1,0:T(8,128)(2,1)S(1)}, u32[]{:S(2)}, u32[]{:S(2)}) async-start(bf16[4,272,128]{2,1,0:T(8,128)(2,1)} %get-tuple-element.27), calls=%async_computation | async-start | bytes 557056 | tf_op jit(solution)/shard_map/all_to_all | solution.py:519
  92.3 13.6 %all-to-all-start.1 = ((f32[16,2,128]{2,1,0:T(2,128)}), f32[16,2,128]{2,1,0:T(2,128)S(1)}, u32[]{:S(2)}, u32[]{:S(2)}) async-start(f32[16,2,128]{2,1,0:T(2,128)} %get-tuple-element.34), calls=%async_computation.1 | async-start | bytes 32768 | tf_op jit(solution)/shard_map/all_to_all | solution.py:530
  105.9 0.6 copy-start
Sparse Core Ops, SparseCore 0:
  10.1 39.5 all-gather.3
  51.9 42.8 all-gather.5

commit v4 on v3

--- a/solution.py
+++ b/solution.py
@@ -302,18 +302,23 @@
 
 
 def norm_kernel(count, mixed_hbm, squares_ref, gain_hbm, out_hbm, mixed_ref, gain_ref, out_ref, sems):
-    finish(begin([(mixed_hbm, mixed_ref), (gain_hbm, gain_ref)], sems))
+    loads = begin([(gain_hbm, gain_ref)] + [(mixed_hbm.at[h], mixed_ref.at[h]) for h in range(HEADS_DEV)], sems)
     total = jnp.sum(squares_ref[...], axis=0)
     inv = lax.rsqrt(total * (1.0 / count) + 1e-05)
     t_ids = lax.broadcasted_iota(jnp.int32, (HD, HD), 0)
     s_ids = lax.broadcasted_iota(jnp.int32, (HD, HD), 1)
+    factors = []
     for half in range(TOK // HD):
         diag = jnp.where(t_ids == s_ids, jnp.broadcast_to(inv[half : half + 1, :], (HD, HD)), 0.0)
-        col = jnp.sum(diag, axis=1, keepdims=True)
-        rows = slice(half * HD, (half + 1) * HD)
-        for h in range(HEADS_DEV):
-            out_ref[h, rows, :] = (mixed_ref[h, rows, :] * col * gain_ref[h : h + 1, :]).astype(BF16)
-    finish(begin([(out_ref, out_hbm)], sems, 2))
+        factors.append(jnp.broadcast_to(jnp.sum(diag, axis=1, keepdims=True), (HD, HD)))
+    factor = jnp.concatenate(factors, axis=0)
+    loads[0].wait()
+    stores = []
+    for h in range(HEADS_DEV):
+        loads[1 + h].wait()
+        out_ref[h] = (mixed_ref[h] * factor * gain_ref[h : h + 1, :]).astype(BF16)
+        stores += begin([(out_ref.at[h], out_hbm.at[h])], sems, 1 + HEADS_DEV + h)
+    finish(stores)
 
 
 def lightning_norm(count, mixed, squares, gain):
@@ -324,7 +329,7 @@
         [HBM, VMEM, HBM],
         [(LIN, BF16, HBM)],
         [(LIN, F32), ((HEADS_DEV, HD), F32), (LIN, BF16)],
-        3,
+        1 + 2 * HEADS_DEV,
     )
 
 
@@ -339,6 +344,20 @@
 
 def wide(stat, width):
     return jnp.concatenate([stat] * (width // HD), axis=1)
+
+
+def by_head(score, soften, fold):
+    ahead, held = score(0), None
+    for h in range(HEADS_DEV + 1):
+        fresh = None
+        if h < HEADS_DEV:
+            raw = ahead
+            if h + 1 < HEADS_DEV:
+                ahead = score(h + 1)
+            fresh = soften(h, raw)
+        if held is not None:
+            fold(h - 1, held)
+        held = fresh
 
 
 def near_kernel(
@@ -381,26 +400,35 @@
     values = with_ones(kv[:, KROWS:PAY, :].reshape(N_YC * KROWS, HD))
     column_keys = kr[:, 0:KROWS, :].reshape((N_Z - 1) * KROWS, HD)
     column_values = with_ones(kr[:, KROWS:PAY, :].reshape((N_Z - 1) * KROWS, HD))
-    for h in range(HEADS_DEV):
-        raw = dot(q_ref[h], keys, NT)
+
+    def score(h):
+        return dot(q_ref[h], keys, NT), dot(q_ref[h], column_keys, NT)
+
+    def soften(h, raws):
+        raw, column_raw = raws
         pieces = []
         for r in range(N_YC):
             span = raw[:, r * KROWS : r * KROWS + TOK]
             pieces.append(jnp.where(ahead <= (place - r) * TOK, span, MASK_FILL))
             pieces.append(raw[:, r * KROWS + TOK : (r + 1) * KROWS] + bias[r])
         raw = jnp.concatenate(pieces, axis=1)
-        column_raw = dot(q_ref[h], column_keys, NT) + line
+        column_raw = column_raw + line
         peak = jnp.maximum(
             jnp.max(raw, axis=1, keepdims=True), jnp.max(column_raw, axis=1, keepdims=True)
         )
         peak = jnp.broadcast_to(peak, (TOK, HD))
+        m_ref[h] = peak
         probs = jnp.exp2((raw - wide(peak, raw.shape[1])) * scale).astype(BF16)
         column_probs = jnp.exp2((column_raw - wide(peak, column_raw.shape[1])) * scale).astype(BF16)
-        m_ref[h] = peak
-        acc_ref[h] = dot(probs, values, NN) + dot(column_probs, column_values, NN)
-        stores += begin(
-            [(m_ref.at[h], m_hbm.at[h]), (acc_ref.at[h], acc_hbm.at[h])], sems, n_loads + 2 + 2 * h
+        return probs, column_probs
+
+    def fold(h, probs):
+        acc_ref[h] = dot(probs[0], values, NN) + dot(probs[1], column_values, NN)
+        stores.extend(
+            begin([(m_ref.at[h], m_hbm.at[h]), (acc_ref.at[h], acc_hbm.at[h])], sems, n_loads + 2 + 2 * h)
         )
+
+    by_head(score, soften, fold)
     finish(stores)
 
 
@@ -430,22 +458,37 @@
     place = ctx_place() % N_YC
     others = [(place + 1 + j) % N_YC for j in range(N_FAR)]
     loads = begin([(q_hbm, q_ref), (m_hbm, m_ref), (acc_hbm, acc_ref)], sems)
-    blocks = []
+
+    def shards(i):
+        pairs = [(kv_hbm.at[r, i], kv.at[i, j]) for j, r in enumerate(others)]
+        return begin(pairs, sems, 3 + i * N_FAR)
+
+    blocks = [shards(0)]
+    finish(loads)
+    finish(blocks[0])
+    blocks += [shards(i) for i in range(1, N_Z - 1)]
+
+    def update(keys, values, mask):
+        def score(h):
+            return dot(q_ref[h], keys, NT)
+
+        def soften(h, raw):
+            raw = mask(raw)
+            m_old = m_ref[h]
+            m_new = jnp.maximum(m_old, jnp.max(raw, axis=1, keepdims=True))
+            m_ref[h] = m_new
+            probs = jnp.exp2((raw - wide(m_new, raw.shape[1])) * scale).astype(BF16)
+            return probs, jnp.exp2((m_old - m_new) * scale)
+
+        def fold(h, held):
+            probs, alpha = held
+            acc_ref[h] = acc_ref[h] * wide(alpha, 2 * HD) + dot(probs, values, NN)
+
+        by_head(score, soften, fold)
+
     for i in range(N_Z - 1):
-        pairs = [(kv_hbm.at[r, i], kv.at[i, j]) for j, r in enumerate(others)]
-        blocks.append(begin(pairs, sems, 3 + i * N_FAR))
-    finish(loads)
-
-    def update(h, raw, values):
-        m_old = m_ref[h]
-        m_new = jnp.maximum(m_old, jnp.max(raw, axis=1, keepdims=True))
-        probs = jnp.exp2((raw - wide(m_new, raw.shape[1])) * scale)
-        alpha = jnp.exp2((m_old - m_new) * scale)
-        m_ref[h] = m_new
-        acc_ref[h] = acc_ref[h] * wide(alpha, 2 * HD) + dot(probs.astype(BF16), values, NN)
-
-    for i in range(N_Z - 1):
-        finish(blocks[i])
+        if i > 0:
+            finish(blocks[i])
         z = (z_place + 1 + i) % N_Z
         bias = [cache_bias(len_ref, z, r) for r in others]
 
@@ -453,21 +496,22 @@
         def whole():
             keys = kv[i, :, 0:KROWS, :].reshape(N_FAR * KROWS, HD)
             values = with_ones(kv[i, :, KROWS:PAY, :].reshape(N_FAR * KROWS, HD))
-            for h in range(HEADS_DEV):
-                raw = dot(q_ref[h], keys, NT)
+
+            def mask(raw):
                 pieces = []
                 for r in range(N_FAR):
                     pieces.append(raw[:, r * KROWS : r * KROWS + TOK])
                     pieces.append(raw[:, r * KROWS + TOK : (r + 1) * KROWS] + bias[r])
-                update(h, jnp.concatenate(pieces, axis=1), values)
+                return jnp.concatenate(pieces, axis=1)
+
+            update(keys, values, mask)
 
         @pl.when(z > z_place)
         def cache_only():
             keys = kv[i, :, TOK:KROWS, :].reshape(N_FAR * CROWS, HD)
             values = with_ones(kv[i, :, KROWS + TOK : PAY, :].reshape(N_FAR * CROWS, HD))
             line = jnp.concatenate(bias, axis=1)
-            for h in range(HEADS_DEV):
-                update(h, dot(q_ref[h], keys, NT) + line, values)
+            update(keys, values, lambda raw: raw + line)
 
     stores = []
     for h in range(HEADS_DEV):

time: 117 us -> 116 us (level)
  transfers between devices with their start and end apart: 4 -> 4, of which waited for: 1 -> 1; matrix products, arithmetic and copies ran while one was open for 0% -> 0% of each run, Pallas kernels for 25% -> 24%
where the time goes in v4:
time: 116 us; the launch traced here: 115 us
  blocking collectives  46.5 us (40%)
  Pallas kernels  33.4 us (29%)
  starting transfers between devices  15.4 us (13%)
  between operations  14.1 us (12%)
  waiting for transfers between devices  5.45 us (5%)
    all_gather x1, blocking collectives, per_device(): lax.all_gather(payload, 'ctx', axis=0, tiled=True, axis_index_groups=Z_GR...  39.1 us
    pallas_call x7, Pallas kernels, run(): pl.pallas_call(kernel, out_shape=shapes[0] if single else shapes, in_spec...  33.4 us
    all_to_all x1, starting transfers between devices, per_device(): lax.all_to_all(plane_totals, 'ctx', 0, 0, axis_index_groups=Z_GROUPS)  10.6 us
    all_gather x1, blocking collectives, per_device(): lax.all_gather(totals, 'ctx', axis=0, axis_index_groups=CORE_GROUPS)  7.4 us
    all_to_all x1, waiting for transfers between devices, per_device(): lax.all_to_all(plane_totals, 'ctx', 0, 0, axis_index_groups=Z_GROUPS)  5.37 us
    all_to_all x1, starting transfers between devices, per_device(): all_squares = lax.all_to_all(squares, 'tp', 0, 0)  4.67 us
  transfers between devices with their start and end apart: 4, of which 1 were waited for; matrix products, arithmetic and copies ran while one was open for 0% of the time, Pallas kernels for 24%

profile of v4, /device:TPU:1, one launch (start us, length us, event | category | flops | bytes accessed | tf_op | source)
XLA Modules:
  0.0 115.4 jit_solution(9255179225536091338)
XLA Ops:
  7.2 0.0 all-gather.4.cloned.1.call-start
  7.2 2.7 %prep.1 = (bf16[768,128]{1,0:T(8,128)(2,1)}, bf16[1296,128]{1,0:T(8,128)(2,1)}) custom-call(bf16[8,256,128]{2,1,0:T(8,128)(2,1)} %sk_hbm.1, bf16[8,256,128]{2,1,0:T(8,128)(2,1)} %sv_hbm.1, bf16[8,128,128]{2,1,0:T(8,128)(2,1)} %ck_hbm.1, bf16[8,128,128]{2,1,0:T(8,128)(2,1)} %cv_hbm.1, bf16[4,256,128]{2,1,0:T(8,128)(2,1)} %lk_hbm.1, ...), custom_call_target="tpu_custom_call" | custom-call | tf_op jit(solution)/shard_map/prep/pallas_call | solution.py:87
  9.9 0.0 all-gather.4.cloned.1.call-update
  9.9 0.0 all-gather.6.cloned.1.call-start
  10.0 39.1 %all_gather.16 = bf16[3072,128]{1,0:T(8,128)(2,1)} all-gather(bf16[768,128]{1,0:T(8,128)(2,1)} %get-tuple-element.20), channel_id=1, replica_groups={{0,128,256,384},{16,144,272,400},{32,160,288,416},{48,176,304,432},{64,..., dimensions={0}, use_global_device_ids=true | all-gather | bytes 983040 | tf_op jit(solution)/shard_map/all_gather | solution.py:555
  49.1 1.9 %other_planes.1.rest_hbm = bf16[3,768,128]{2,1,0:T(8,128)(2,1)} custom-call(bf16[4,768,128]{2,1,0:T(8,128)(2,1)} %bitcast.9), custom_call_target="tpu_custom_call" | custom-call | tf_op jit(solution)/shard_map/other_planes/pallas_call | solution.py:87
  51.0 0.0 all-gather.6.cloned.1.call-update
  51.0 0.0 all-gather.4.cloned.1.call-done
  51.1 2.9 %plane_scan.1 = (f32[4,128,128]{2,1,0:T(8,128)}, f32[4,128]{1,0:T(4,128)}, bf16[4,272,128]{2,1,0:T(8,128)(2,1)}) custom-call(bf16[8,1296,128]{2,1,0:T(8,128)(2,1)} %bitcast.5), custom_call_target="tpu_custom_call" | custom-call | tf_op jit(solution)/shard_map/plane_scan/pallas_call | solution.py:87
  54.0 10.6 %all-to-all-start = ((bf16[4,272,128]{2,1,0:T(8,128)(2,1)}), bf16[4,272,128]{2,1,0:T(8,128)(2,1)S(1)}, u32[]{:S(2)}, u32[]{:S(2)}) async-start(bf16[4,272,128]{2,1,0:T(8,128)(2,1)} %get-tuple-element.27), calls=%async_computation | async-start | bytes 557056 | tf_op jit(solution)/shard_map/all_to_all | solution.py:563
  64.6 11.0 %near_work.1 = (f32[4,256,128]{2,1,0:T(8,128)}, f32[4,256,256]{2,1,0:T(8,128)}, f32[4,256,128]{2,1,0:T(8,128)}, f32[256,8]{1,0:T(8,128)}) custom-call(s32[32]{0:T(128)} %len_ref.3, bf16[4,256,128]{2,1,0:T(8,128)(2,1)} %q_hbm.5, bf16[8,1296,128]{2,1,0:T(8,128)(2,1)} %bitcast.6, bf16[3,768,128]{2,1,0:T(8,128)(2,1)} %other_planes.1.rest_hbm, ...), custom_call_target="tpu_custom_call" | custom-call | tf_op jit(solution)/shard_map/near_work/pallas_call | solution.py:87
  75.5 5.4 %all-to-all-done = bf16[4,272,128]{2,1,0:T(8,128)(2,1)S(1)} async-done(((bf16[4,272,128]{2,1,0:T(8,128)(2,1)}), bf16[4,272,128]{2,1,0:T(8,128)(2,1)S(1)}, u32[]{:S(2)}, u32[]{:S(2)}) %all-to-all-start) | async-done | bytes 278560 | tf_op jit(solution)/shard_map/all_to_all | solution.py:563
  80.9 7.4 %all-gather = bf16[8,272,128]{2,1,0:T(8,128)(2,1)} all-gather(bf16[4,272,128]{2,1,0:T(8,128)(2,1)S(1)} %all-to-all-done), channel_id=2, replica_groups={{0,16},{32,48},{64,80},{96,112},{128,144},{160,176},{192,208},{224,240}..., dimensions={0}, use_global_device_ids=true | all-gather | bytes 835584 | tf_op jit(solution)/shard_map/all_gather | solution.py:564
  88.3 4.0 %lightning_mix.1 = (f32[4,256,128]{2,1,0:T(8,128)}, f32[16,2,128]{2,1,0:T(2,128)}) custom-call(bf16[4,256,128]{2,1,0:T(8,128)(2,1)} %q_hbm.4, f32[4,256,128]{2,1,0:T(8,128)} %get-tuple-element.21.mixed_hbm, f32[256,8]{1,0:T(8,128)} %get-tuple-element.22.cum_hbm, f32[4,128,128]{2,1,0:T(8,128)} %get-tuple-element.25.own_hbm, ...), custom_call_target="tpu_custom_call" | custom-call | tf_op jit(solution)/shard_map/lightning_mix/pallas_call | solution.py:87
  92.3 4.7 %all-to-all-start.1 = ((f32[16,2,128]{2,1,0:T(2,128)}), f32[16,2,128]{2,1,0:T(2,128)S(1)}, u32[]{:S(2)}, u32[]{:S(2)}) async-start(f32[16,2,128]{2,1,0:T(2,128)} %get-tuple-element.34), calls=%async_computation.1 | async-start | bytes 32768 | tf_op jit(solution)/shard_map/all_to_all | solution.py:574
  97.0 0.0 all-gather.6.cloned.1.call-done
  97.0 8.4 %far_attention.1 = bf16[4,256,128]{2,1,0:T(8,128)(2,1)} custom-call(s32[32]{0:T(128)} %len_ref.3, bf16[4,256,128]{2,1,0:T(8,128)(2,1)} %q_hbm.5, f32[4,256,128]{2,1,0:T(8,128)} %get-tuple-element.31.m_hbm, f32[4,256,256]{2,1,0:T(8,128)} %get-tuple-element.32.acc_hbm, bf16[8,3,768,128]{3,2,1,0:T(8,128)(2,1)} %bitcast.8), custom_call_target="tpu_custom_call" | custom-call | tf_op jit(solution)/shard_map/far_attention/pallas_call | solution.py:87
  105.4 0.0 all-to-all-done.1.squares_ref
  105.4 0.0 copy-start
  105.4 0.6 copy-done
  106.0 2.5 %lightning_norm.1 = bf16[4,256,128]{2,1,0:T(8,128)(2,1)} custom-call(f32[4,256,128]{2,1,0:T(8,128)} %get-tuple-element.33.mixed_hbm, f32[16,2,128]{2,1,0:T(2,128)} %copy-done, f32[4,128]{1,0:T(4,128)} %gain_hbm.1), custom_call_target="tpu_custom_call" | custom-call | tf_op jit(solution)/shard_map/lightning_norm/pallas_call | solution.py:87
Async XLA Ops:
  7.2 43.9 %all-gather.4.cloned.1.call-start = ((), (), s32[]{:S(2)}) async-start(), calls=%async_computation.2 | async-start | bytes 2985984 | tf_op jit(solution)/shard_map/all_gather | solution.py:553
  9.9 87.0 %all-gather.6.cloned.1.call-start = ((), (), s32[]{:S(2)}) async-start(), calls=%async_computation.3 | async-start | bytes 5308416 | tf_op jit(solution)/shard_map/all_gather | solution.py:557
  54.0 26.9 %all-to-all-start = ((bf16[4,272,128]{2,1,0:T(8,128)(2,1)}), bf16[4,272,128]{2,1,0:T(8,128)(2,1)S(1)}, u32[]{:S(2)}, u32[]{:S(2)}) async-start(bf16[4,272,128]{2,1,0:T(8,128)(2,1)} %get-tuple-element.27), calls=%async_computation | async-start | bytes 557056 | tf_op jit(solution)/shard_map/all_to_all | solution.py:563
  92.3 13.1 %all-to-all-start.1 = ((f32[16,2,128]{2,1,0:T(2,128)}), f32[16,2,128]{2,1,0:T(2,128)S(1)}, u32[]{:S(2)}, u32[]{:S(2)}) async-start(f32[16,2,128]{2,1,0:T(2,128)} %get-tuple-element.34), calls=%async_computation.1 | async-start | bytes 32768 | tf_op jit(solution)/shard_map/all_to_all | solution.py:574
  105.4 0.6 copy-start
Sparse Core Ops, SparseCore 0:
  10.1 39.5 all-gather.3
  51.9 42.8 all-gather.5

commit v5 on v4

--- a/solution.py
+++ b/solution.py
@@ -256,8 +256,9 @@
     )
     place = ctx_place()
     z_place = place // N_YC
-    finish(loads)
+    finish(loads[:3])
     stores = []
+    late = loads[3:]
     total = jnp.zeros((TOK, HD), F32)
     for h in range(HEADS_DEV):
         core, inner = h // HEADS_CORE, h % HEADS_CORE
@@ -270,8 +271,13 @@
         state = own_ref[h] + jnp.exp(own_decay_ref[h : h + 1, :]) * acc
         state = jnp.where(place == 0, prior_ref[h], state)
         hi, low = split2(state)
+        if h == 0:
+            late[1].wait()
         q = q_ref[h]
         inter = dot(q, hi, NN) + dot(q, low, NN)
+        if h == 0:
+            late[0].wait()
+            late[2].wait()
         mixed = mixed_ref[h] + jnp.exp(cum_ref[:, h : h + 1]) * inter
         out_ref[h] = mixed
         stores += begin([(out_ref.at[h], out_hbm.at[h])], sems, 6 + h)

time: 116 us -> 116 us (level)
  no operation moved by 1% of the time
where the time goes in v5:
time: 116 us; the launch traced here: 115 us
  blocking collectives  46.5 us (40%)
  Pallas kernels  33.3 us (29%)
  starting transfers between devices  15.4 us (13%)
  between operations  14.1 us (12%)
  waiting for transfers between devices  5.45 us (5%)
    all_gather x1, blocking collectives, per_device(): lax.all_gather(payload, 'ctx', axis=0, tiled=True, axis_index_groups=Z_GR...  39.1 us
    pallas_call x7, Pallas kernels, run(): pl.pallas_call(kernel, out_shape=shapes[0] if single else shapes, in_spec...  33.3 us
    all_to_all x1, starting transfers between devices, per_device(): lax.all_to_all(plane_totals, 'ctx', 0, 0, axis_index_groups=Z_GROUPS)  10.6 us
    all_gather x1, blocking collectives, per_device(): lax.all_gather(totals, 'ctx', axis=0, axis_index_groups=CORE_GROUPS)  7.4 us
    all_to_all x1, waiting for transfers between devices, per_device(): lax.all_to_all(plane_totals, 'ctx', 0, 0, axis_index_groups=Z_GROUPS)  5.37 us
    all_to_all x1, starting transfers between devices, per_device(): all_squares = lax.all_to_all(squares, 'tp', 0, 0)  4.68 us
  transfers between devices with their start and end apart: 4, of which 1 were waited for; matrix products, arithmetic and copies ran while one was open for 0% of the time, Pallas kernels for 24%

profile of v5, /device:TPU:1, one launch (start us, length us, event | category | flops | bytes accessed | tf_op | source)
XLA Modules:
  0.0 115.4 jit_solution(11953566294618403036)
XLA Ops:
  7.2 0.0 all-gather.4.cloned.1.call-start
  7.2 2.7 %prep.1 = (bf16[768,128]{1,0:T(8,128)(2,1)}, bf16[1296,128]{1,0:T(8,128)(2,1)}) custom-call(bf16[8,256,128]{2,1,0:T(8,128)(2,1)} %sk_hbm.1, bf16[8,256,128]{2,1,0:T(8,128)(2,1)} %sv_hbm.1, bf16[8,128,128]{2,1,0:T(8,128)(2,1)} %ck_hbm.1, bf16[8,128,128]{2,1,0:T(8,128)(2,1)} %cv_hbm.1, bf16[4,256,128]{2,1,0:T(8,128)(2,1)} %lk_hbm.1, ...), custom_call_target="tpu_custom_call" | custom-call | tf_op jit(solution)/shard_map/prep/pallas_call | solution.py:87
  9.9 0.0 all-gather.4.cloned.1.call-update
  9.9 0.0 all-gather.6.cloned.1.call-start
  10.0 39.1 %all_gather.16 = bf16[3072,128]{1,0:T(8,128)(2,1)} all-gather(bf16[768,128]{1,0:T(8,128)(2,1)} %get-tuple-element.20), channel_id=1, replica_groups={{0,128,256,384},{16,144,272,400},{32,160,288,416},{48,176,304,432},{64,..., dimensions={0}, use_global_device_ids=true | all-gather | bytes 983040 | tf_op jit(solution)/shard_map/all_gather | solution.py:561
  49.1 1.9 %other_planes.1.rest_hbm = bf16[3,768,128]{2,1,0:T(8,128)(2,1)} custom-call(bf16[4,768,128]{2,1,0:T(8,128)(2,1)} %bitcast.9), custom_call_target="tpu_custom_call" | custom-call | tf_op jit(solution)/shard_map/other_planes/pallas_call | solution.py:87
  51.0 0.0 all-gather.6.cloned.1.call-update
  51.0 0.0 all-gather.4.cloned.1.call-done
  51.1 2.9 %plane_scan.1 = (f32[4,128,128]{2,1,0:T(8,128)}, f32[4,128]{1,0:T(4,128)}, bf16[4,272,128]{2,1,0:T(8,128)(2,1)}) custom-call(bf16[8,1296,128]{2,1,0:T(8,128)(2,1)} %bitcast.5), custom_call_target="tpu_custom_call" | custom-call | tf_op jit(solution)/shard_map/plane_scan/pallas_call | solution.py:87
  54.0 10.6 %all-to-all-start = ((bf16[4,272,128]{2,1,0:T(8,128)(2,1)}), bf16[4,272,128]{2,1,0:T(8,128)(2,1)S(1)}, u32[]{:S(2)}, u32[]{:S(2)}) async-start(bf16[4,272,128]{2,1,0:T(8,128)(2,1)} %get-tuple-element.27), calls=%async_computation | async-start | bytes 557056 | tf_op jit(solution)/shard_map/all_to_all | solution.py:569
  64.6 11.0 %near_work.1 = (f32[4,256,128]{2,1,0:T(8,128)}, f32[4,256,256]{2,1,0:T(8,128)}, f32[4,256,128]{2,1,0:T(8,128)}, f32[256,8]{1,0:T(8,128)}) custom-call(s32[32]{0:T(128)} %len_ref.3, bf16[4,256,128]{2,1,0:T(8,128)(2,1)} %q_hbm.5, bf16[8,1296,128]{2,1,0:T(8,128)(2,1)} %bitcast.6, bf16[3,768,128]{2,1,0:T(8,128)(2,1)} %other_planes.1.rest_hbm, ...), custom_call_target="tpu_custom_call" | custom-call | tf_op jit(solution)/shard_map/near_work/pallas_call | solution.py:87
  75.5 5.4 %all-to-all-done = bf16[4,272,128]{2,1,0:T(8,128)(2,1)S(1)} async-done(((bf16[4,272,128]{2,1,0:T(8,128)(2,1)}), bf16[4,272,128]{2,1,0:T(8,128)(2,1)S(1)}, u32[]{:S(2)}, u32[]{:S(2)}) %all-to-all-start) | async-done | bytes 278560 | tf_op jit(solution)/shard_map/all_to_all | solution.py:569
  80.9 7.4 %all-gather = bf16[8,272,128]{2,1,0:T(8,128)(2,1)} all-gather(bf16[4,272,128]{2,1,0:T(8,128)(2,1)S(1)} %all-to-all-done), channel_id=2, replica_groups={{0,16},{32,48},{64,80},{96,112},{128,144},{160,176},{192,208},{224,240}..., dimensions={0}, use_global_device_ids=true | all-gather | bytes 835584 | tf_op jit(solution)/shard_map/all_gather | solution.py:570
  88.3 3.9 %lightning_mix.1 = (f32[4,256,128]{2,1,0:T(8,128)}, f32[16,2,128]{2,1,0:T(2,128)}) custom-call(bf16[4,256,128]{2,1,0:T(8,128)(2,1)} %q_hbm.4, f32[4,256,128]{2,1,0:T(8,128)} %get-tuple-element.21.mixed_hbm, f32[256,8]{1,0:T(8,128)} %get-tuple-element.22.cum_hbm, f32[4,128,128]{2,1,0:T(8,128)} %get-tuple-element.25.own_hbm, ...), custom_call_target="tpu_custom_call" | custom-call | tf_op jit(solution)/shard_map/lightning_mix/pallas_call | solution.py:87
  92.3 4.7 %all-to-all-start.1 = ((f32[16,2,128]{2,1,0:T(2,128)}), f32[16,2,128]{2,1,0:T(2,128)S(1)}, u32[]{:S(2)}, u32[]{:S(2)}) async-start(f32[16,2,128]{2,1,0:T(2,128)} %get-tuple-element.34), calls=%async_computation.1 | async-start | bytes 32768 | tf_op jit(solution)/shard_map/all_to_all | solution.py:580
  97.0 0.0 all-gather.6.cloned.1.call-done
  97.0 8.4 %far_attention.1 = bf16[4,256,128]{2,1,0:T(8,128)(2,1)} custom-call(s32[32]{0:T(128)} %len_ref.3, bf16[4,256,128]{2,1,0:T(8,128)(2,1)} %q_hbm.5, f32[4,256,128]{2,1,0:T(8,128)} %get-tuple-element.31.m_hbm, f32[4,256,256]{2,1,0:T(8,128)} %get-tuple-element.32.acc_hbm, bf16[8,3,768,128]{3,2,1,0:T(8,128)(2,1)} %bitcast.8), custom_call_target="tpu_custom_call" | custom-call | tf_op jit(solution)/shard_map/far_attention/pallas_call | solution.py:87
  105.4 0.0 all-to-all-done.1.squares_ref
  105.4 0.0 copy-start
  105.4 0.6 copy-done
  106.0 2.5 %lightning_norm.1 = bf16[4,256,128]{2,1,0:T(8,128)(2,1)} custom-call(f32[4,256,128]{2,1,0:T(8,128)} %get-tuple-element.33.mixed_hbm, f32[16,2,128]{2,1,0:T(2,128)} %copy-done, f32[4,128]{1,0:T(4,128)} %gain_hbm.1), custom_call_target="tpu_custom_call" | custom-call | tf_op jit(solution)/shard_map/lightning_norm/pallas_call | solution.py:87
Async XLA Ops:
  7.2 43.9 %all-gather.4.cloned.1.call-start = ((), (), s32[]{:S(2)}) async-start(), calls=%async_computation.2 | async-start | bytes 2985984 | tf_op jit(solution)/shard_map/all_gather | solution.py:559
  9.9 87.0 %all-gather.6.cloned.1.call-start = ((), (), s32[]{:S(2)}) async-start(), calls=%async_computation.3 | async-start | bytes 5308416 | tf_op jit(solution)/shard_map/all_gather | solution.py:563
  54.0 26.9 %all-to-all-start = ((bf16[4,272,128]{2,1,0:T(8,128)(2,1)}), bf16[4,272,128]{2,1,0:T(8,128)(2,1)S(1)}, u32[]{:S(2)}, u32[]{:S(2)}) async-start(bf16[4,272,128]{2,1,0:T(8,128)(2,1)} %get-tuple-element.27), calls=%async_computation | async-start | bytes 557056 | tf_op jit(solution)/shard_map/all_to_all | solution.py:569
  92.3 13.1 %all-to-all-start.1 = ((f32[16,2,128]{2,1,0:T(2,128)}), f32[16,2,128]{2,1,0:T(2,128)S(1)}, u32[]{:S(2)}, u32[]{:S(2)}) async-start(f32[16,2,128]{2,1,0:T(2,128)} %get-tuple-element.34), calls=%async_computation.1 | async-start | bytes 32768 | tf_op jit(solution)/shard_map/all_to_all | solution.py:580
  105.4 0.6 copy-start
Sparse Core Ops, SparseCore 0:
  10.1 39.5 all-gather.3
  51.9 42.8 all-gather.5
